TPU v7x, 256 devices: a whole 4x4x8 slice. The times are simulated.
256 devices in a mesh: row: 16 (over y, x), col: 16 (over z, core).
Axes of the slice: x: 4, y: 4, z: 8, core: 2. Of those that a mesh axis runs over, the one named last changes fastest.
Arguments:
- matrix: float32 [2, 4096, 2, 4096], P(None, 'row', None, 'col'), may hold values from -8 to 8, as said below
Outputs:
- reduced: float32 [2, 4096, 2, 4096], P(None, 'row', None, 'col')
Inputs may be any that keep to these rules, and one draw needn't show every extreme that they name: symmetric: the entries at (r, c) and (c, r) of the 8192 x 8192 matrix are equal.
All inputs are finite; a program needn't handle non-finite values.
Results may differ from a plain program's by a relative error of at most 0.0002.
Values sent between devices are 32-bit elements; how exact they have to be, the bound alone decides.
No kernel may reach another device: no remote copies, remote signals or barrier semaphores. Data moves between devices by JAX's collectives and lax.ppermute only.
A program may use at most 64 MiB of HBM per device.

v0:
```python
import functools

import jax
import jax.numpy as jnp
from jax import lax
from jax.experimental import pallas as pl
from jax.experimental.pallas import tpu as pltpu
from jax.sharding import Mesh
from jax.sharding import PartitionSpec as P

PANELS = 2
COL = ("col_0", "col_1")

highest = lax.Precision.HIGHEST
high = lax.Precision.HIGH


def product(left, right, dims=((1,), (0,)), precision=high):
    return lax.dot_general(
        left, right, (dims, ((), ())), precision=precision, preferred_element_type=jnp.float32
    )


NT = ((1,), (1,))
TN = ((0,), (0,))
GROUP = 8


def row_of(tile, s):
    return jnp.broadcast_to(tile[s : s + 1, :], (8, 128))


class Elimination:
    def __init__(self, window, off, b):
        self.b, self.off, self.count = b, off, b // 8
        self.sublane = lax.broadcasted_iota(jnp.int32, (8, 128), 0)
        lanes = lax.broadcasted_iota(jnp.int32, (8, 128), 1)
        self.a = [window[8 * i : 8 * i + 8, :] for i in range(self.count)]
        self.e = [(lanes == self.sublane + 8 * i).astype(jnp.float32) for i in range(self.count)]
        zero = jnp.zeros((8, 128), jnp.float32)
        self.low = [zero] * self.count
        self.inv = [zero] * self.count

    def group(self, t):
        tiles = range(self.count)
        first = self.off + GROUP * t
        cols = [
            [jnp.broadcast_to(self.a[i][:, first + q : first + q + 1], (8, 128)) for i in tiles]
            for q in range(GROUP)
        ]
        for q in range(GROUP):
            inv = 1.0 / row_of(cols[q][t], q)
            here = self.sublane == q
            scale = [cols[q][i] * inv for i in tiles]
            scale[t] = jnp.where(here, 0.0, scale[t])
            for p in range(q + 1, GROUP):
                head = row_of(cols[p][t], q)
                for i in tiles:
                    cols[p][i] = cols[p][i] - scale[i] * head
            self.inv[t] = jnp.where(here, inv, self.inv[t])
            self.low[t] = jnp.where(here, self.e[t], self.low[t])
            row_a = row_of(self.a[t], q)
            row_e = row_of(self.e[t], q)
            for i in tiles:
                self.a[i] = self.a[i] - scale[i] * row_a
                self.e[i] = self.e[i] - scale[i] * row_e

    def inverse(self):
        inv = jnp.concatenate(self.inv, axis=0)
        return (jnp.concatenate(self.e, axis=0) * inv)[:, : self.b]

    def lower_inverse(self):
        inv = jnp.concatenate(self.inv, axis=0)
        return (jnp.concatenate(self.low, axis=0) * jnp.sqrt(inv))[:, : self.b]


def factor_kernel(g_ref, x_ref, r_ref, t_ref, aa, xb, wb, *, b):
    exact = functools.partial(product, precision=highest)
    n = g_ref.shape[0]
    count = n // b
    rows = lax.broadcasted_iota(jnp.int32, (n, n), 0)
    cols = lax.broadcasted_iota(jnp.int32, (n, n), 1)
    aa[:, :n] = g_ref[...]
    aa[:, n:] = (rows == cols).astype(jnp.float32)
    xb[:, :n] = x_ref[...]
    xb[:, n:] = jnp.zeros((n, n), jnp.float32)
    wb[...] = jnp.zeros((128, 2 * n), jnp.float32)
    lane = lax.broadcasted_iota(jnp.int32, (n, 128), 1)
    row = lax.broadcasted_iota(jnp.int32, (n, 128), 0)
    second = None
    for k in range(count + 1):
        lo, hi = k * b, (k + 1) * b
        win, off = lo // 128 * 128, lo % 128
        running = []
        if k < count:
            first = Elimination(aa[lo:hi, win : win + 128], off, b)
            running.append(first)
        if k > 0:
            second = Elimination(pivot, (lo - b) % 128, b)
            running.append(second)
        for t in range(b // 8):
            for one in running:
                one.group(t)
        if k < count:
            block = aa[lo:hi, :]
            if hi < n:
                wb[off : off + b, :] = exact(first.inverse(), block)
                keep = (lane[: n - hi] >= off) & (lane[: n - hi] < off + b)
                left = jnp.where(keep, aa[hi:, win : win + 128], 0.0)
                aa[hi:, :] = aa[hi:, :] - exact(left, wb[...])
            upper = exact(first.lower_inverse(), block)
            wide_row = lax.broadcasted_iota(jnp.int32, (b, 2 * n), 0) + lo
            wide_col = lax.broadcasted_iota(jnp.int32, (b, 2 * n), 1)
            upper = jnp.where(wide_col >= wide_row, upper, 0.0)
            upper = jnp.where(wide_col - n > wide_row, 0.0, upper)
            r_ref[lo:hi, :] = upper[:, :n]
        if k > 0:
            plo, phi = lo - b, lo
            pwin, poff = plo // 128 * 128, plo % 128
            xb[plo:phi, :] = exact(second.inverse(), pivot_row)
            keep = (lane >= poff) & (lane < poff + b) & ((row < plo) | (row >= phi))
            left = jnp.where(keep, xb[:, pwin : pwin + 128], 0.0)
            xb[...] = xb[...] - exact(left, xb[pwin : pwin + 128, :])
        if k < count:
            pivot_row = xb[lo:hi, :] + upper
            pivot = pivot_row[:, win : win + 128]
    t_ref[...] = xb[:, n:]


def factor(gram, top):
    n = gram.shape[0]
    square = jax.ShapeDtypeStruct((n, n), jnp.float32)
    return pl.pallas_call(
        functools.partial(factor_kernel, b=32),
        out_shape=(square, square),
        scratch_shapes=[
            pltpu.VMEM((n, 2 * n), jnp.float32),
            pltpu.VMEM((n, 2 * n), jnp.float32),
            pltpu.VMEM((128, 2 * n), jnp.float32),
        ],
        name="factor",
    )(gram, top)


def exchange(value, axis):
    return lax.all_to_all(value, axis, 0, 0, tiled=True)


def copied(value, axis):
    copies = jnp.broadcast_to(value, (lax.axis_size(axis), *value.shape))
    return exchange(copies, axis)


def transposed(value):
    rows = lax.axis_size("row")
    cols = lax.axis_size(COL)
    pairs = [(r * cols + c, c * rows + r) for r in range(rows) for c in range(cols)]
    return lax.ppermute(value, ("row", *COL), pairs)


def swapped(value):
    return lax.ppermute(value, COL[1], [(0, 1), (1, 0)])


def core_sum(value):
    return value + swapped(value)


def both_cores(lines):
    other = swapped(lines)
    second = lax.axis_index(COL[1]) == 1
    pair = [jnp.where(second, other, lines), jnp.where(second, lines, other)]
    return jnp.stack(pair, axis=1)


def join(parts):
    parts = parts.reshape(-1, *parts.shape[-3:])
    first, last = parts[:, 0], parts[:, 1]
    local = parts.shape[-1]
    return first.reshape(-1, local), last.reshape(-1, local)


def shards(matrix):
    row_blocks, width, _, _ = matrix.shape
    devices = lax.axis_size("row")
    row_index = lax.axis_index("row")
    col_index = lax.axis_index(COL)
    local = row_blocks * width
    part = width // devices
    dense = matrix.reshape(local, local)
    offsets = jnp.arange(local, dtype=jnp.int32)
    global_rows = (offsets // width * devices + row_index) * width + offsets % width
    global_cols = (offsets // width * devices + col_index) * width + offsets % width
    own = row_index * part
    corners = []
    sent = exchange(dense[:width].reshape(devices, part, local), "row")
    for panel in range(PANELS):
        start = (panel + 1) * width
        last = panel + 1 == PANELS
        below_cols = global_cols[None, :] >= start
        gathered = []
        if panel == 0:
            x_own, c_own, *later = [
                jnp.where(below_cols, sent[source], 0.0) for source in range(PANELS + 1)
            ]
            gathered = [transposed(x_own)]
            x_cols = copied(x_own, "row").reshape(width, local)
        x_piece = lax.dynamic_slice_in_dim(x_cols, own, part, 0)
        gram_part = product(x_piece, x_cols, NT, highest)
        top_part = jnp.where(col_index == panel + 1, x_piece[:, :width], 0.0)
        summed = core_sum(jnp.concatenate([gram_part, top_part]))
        lines = copied(jnp.concatenate([summed.reshape(part, local), *gathered]), COL[0])
        sums = jnp.sum(lines[:, :part], axis=0).reshape(2 * part, width)
        if panel == 0:
            x_rows = both_cores(lines[:, part:]).reshape(width, local)
        u_part = product(x_rows, dense)
        shared = jnp.concatenate([sums, c_own.reshape(2 * part, width)])
        merged = jnp.concatenate(
            [
                jnp.broadcast_to(shared, (devices, *shared.shape)),
                u_part.reshape(devices, 2 * part, width),
            ],
            axis=1,
        )
        merged = exchange(merged, "row")
        gram = merged[:, :part].reshape(width, width)
        top = merged[:, part : 2 * part].reshape(width, width).T
        c_cols = merged[:, 2 * part : 4 * part].reshape(width, local)
        u_own = jnp.sum(merged[:, 4 * part :], axis=0).reshape(part, local)
        u_own = jnp.where(below_cols, u_own, 0.0)
        pair = transposed(jnp.stack([u_own, c_own]))
        pair = copied(pair, COL[0])
        upper, core = factor(gram, top)
        pair, upper, core = lax.optimization_barrier((pair, upper, core))
        u_rows, c_rows = join(both_cores(pair))
        lower = upper.T

        def with_top(x, index):
            head = jnp.where(index == panel + 1, lower, 0.0)
            return jnp.concatenate([x[:, :width] + head, x[:, width:]], axis=1)

        v_cols = with_top(x_cols, col_index)
        v_rows = with_top(x_rows, row_index)
        w_own = u_own + product(lax.dynamic_slice_in_dim(lower, own, part, 0), c_cols)
        w_rows = u_rows + product(lower, c_rows)
        parts = [product(w_own, v_cols, NT)]
        if not last:
            across = lax.dynamic_slice_in_dim(x_cols, own, part, 1).T
            parts += [
                jnp.where(col_index == panel + 1, w_own[:, :width], 0.0),
                jnp.where(col_index == panel + 2, w_own[:, :width], 0.0),
                jnp.where(col_index == panel + 2, across, 0.0),
            ]
        sums = jnp.sum(copied(core_sum(jnp.concatenate(parts)), COL[0]), axis=0)
        shared = jnp.concatenate([w_own.reshape(2 * part, width), sums[: 3 * part]])
        shared = copied(shared, "row")
        w_cols = shared[:, : 2 * part].reshape(width, local)
        inner = shared[:, 2 * part : 3 * part].reshape(width, width)
        middle = 0.5 * product(product(core, inner), core, NT)
        y_cols = product(core, w_cols) - product(middle, v_cols)
        y_rows = product(core, w_rows) - product(middle, v_rows)
        dense = dense - product(
            jnp.concatenate([y_rows, v_rows]), jnp.concatenate([v_cols, y_cols]), TN
        )
        corners.append(upper)
        if last:
            break

        def reduced(old, w_t, v, v_others, y_others):
            y = product(w_t, core, ((0,), (1,))) - product(v, middle, NT)
            both = jnp.concatenate([y, v], axis=1)
            return old - product(both, jnp.concatenate([v_others, y_others]))

        w_top = shared[:, 3 * part : 4 * part].reshape(width, width)
        w_next = shared[:, 4 * part :].reshape(width, width)
        w_next = lax.dynamic_slice_in_dim(w_next, own, part, 1)
        v_top = top + upper
        x_cols = reduced(c_cols, w_top, v_top, v_cols, y_cols)
        x_rows = reduced(c_rows, w_top, v_top, v_rows, y_rows)
        c_own = reduced(later[0], w_next, sums[3 * part :], v_cols, y_cols)
        x_cols = jnp.where(global_cols[None, :] >= start + width, x_cols, 0.0)
        x_rows = jnp.where(global_rows[None, :] >= start + width, x_rows, 0.0)
        c_own = jnp.where(global_cols[None, :] >= start + width, c_own, 0.0)
    slot_rows = offsets[:, None] < width
    slot_cols = offsets[None, :] < width
    for panel, upper in enumerate(corners):
        start = (panel + 1) * width
        pad = ((0, local - width), (0, local - width))
        at_cols = (col_index == panel) & slot_cols & (global_rows[:, None] >= start)
        new_cols = jnp.where(row_index == panel + 1, -jnp.pad(upper, pad), 0.0)
        dense = jnp.where(at_cols, new_cols, dense)
        at_rows = (row_index == panel) & slot_rows & (global_cols[None, :] >= start)
        new_rows = jnp.where(col_index == panel + 1, -jnp.pad(upper.T, pad), 0.0)
        dense = jnp.where(at_rows, new_rows, dense)
    return dense.reshape(matrix.shape)


def solution(mesh):
    split = Mesh(mesh.devices.reshape(mesh.shape["row"], 8, 2), ("row", "col_0", "col_1"))
    placed = (P(None, "row", None, COL),)
    return jax.shard_map(
        shards, mesh=split, in_specs=placed, out_specs=P(None, "row", None, COL), check_vma=False
    )
```

profile of v0, /device:TPU:2, one launch (start us, length us, event | category | flops | bytes accessed | tf_op | source)
XLA Modules:
  0.0 353.6 jit_solution(4649778661520033665)
XLA Ops:
  0.0 1.2 slice.113
  1.2 1.2 reshape.260
  2.4 7.5 %all-to-all-start = ((f32[16,16,512]{2,1,0:T(8,128)}), f32[16,16,512]{2,1,0:T(8,128)S(1)}, u32[]{:S(2)}, u32[]{:S(2)}) async-start(f32[16,16,512]{2,1,0:T(8,128)} %reshape.260), calls=%async_computation | async-start | bytes 1048576 | tf_op jit(solution)/shard_map/all_to_all | solution.py:146
  9.9 10.2 %all-to-all-done = f32[16,16,512]{2,1,0:T(8,128)S(1)} async-done(((f32[16,16,512]{2,1,0:T(8,128)}), f32[16,16,512]{2,1,0:T(8,128)S(1)}, u32[]{:S(2)}, u32[]{:S(2)}) %all-to-all-start) | async-done | bytes 524320 | tf_op jit(solution)/shard_map/all_to_all | solution.py:146
  20.1 1.0 broadcast_in_dim.136
  21.1 4.8 %all-to-all-start.1 = ((f32[16,16,512]{2,1,0:T(8,128)}), f32[16,16,512]{2,1,0:T(8,128)S(1)}, u32[]{:S(2)}, u32[]{:S(2)}) async-start(f32[16,16,512]{2,1,0:T(8,128)} %broadcast_in_dim.136), calls=%async_computation.1 | async-start | bytes 1048576 | tf_op jit(solution)/shard_map/all_to_all | solution.py:146
  25.9 9.2 %all-to-all-done.1 = f32[16,16,512]{2,1,0:T(8,128)S(1)} async-done(((f32[16,16,512]{2,1,0:T(8,128)}), f32[16,16,512]{2,1,0:T(8,128)S(1)}, u32[]{:S(2)}, u32[]{:S(2)}) %all-to-all-start.1) | async-done | bytes 524320 | tf_op jit(solution)/shard_map/all_to_all | solution.py:146
  35.7 3.5 collective-permute-start.1
  39.2 1.7 collective-permute-done.1
  41.0 0.9 broadcast_in_dim.138
  41.8 15.8 %all-to-all-start.2 = ((f32[8,32,512]{2,1,0:T(8,128)}), f32[8,32,512]{2,1,0:T(8,128)S(1)}, u32[]{:S(2)}, u32[]{:S(2)}) async-start(f32[8,32,512]{2,1,0:T(8,128)} %broadcast_in_dim.138), calls=%async_computation.2 | async-start | bytes 1048576 | tf_op jit(solution)/shard_map/all_to_all | solution.py:146
  57.8 17.5 %all-to-all-done.2 = f32[8,32,512]{2,1,0:T(8,128)S(1)} async-done(((f32[8,32,512]{2,1,0:T(8,128)}), f32[8,32,512]{2,1,0:T(8,128)S(1)}, u32[]{:S(2)}, u32[]{:S(2)}) %all-to-all-start.2) | async-done | bytes 524320 | tf_op jit(solution)/shard_map/all_to_all | solution.py:146
  77.0 0.8 copy-done.5
  78.8 26.6 %all_to_all.60 = f32[16,96,256]{2,1,0:T(8,128)S(1)} all-to-all(f32[16,96,256]{2,1,0:T(8,128)S(1)} %pad_maximum_fusion), channel_id=1, replica_groups=mesh['row'=16,'col_0'=8,'col_1'=2] {'row'}, dimensions={0} | all-to-all | bytes 3145728 | tf_op jit(solution)/shard_map/all_to_all | solution.py:146
  105.4 0.9 fusion.85
  106.3 2.0 collective-permute-start.3
  108.3 4.2 %collective-permute-done.3 = f32[2,16,512]{2,1,0:T(8,128)S(1)} collective-permute-done((f32[2,16,512]{2,1,0:T(8,128)S(1)}, f32[2,16,512]{2,1,0:T(8,128)S(1)}, u32[]{:S(2)}, u32[]{:S(2)}) %collective-permute-start.3) | collective-permute-done | bytes 65568 | tf_op jit(solution)/shard_map/ppermute | solution.py:158
  112.5 0.9 broadcast_in_dim.145
  113.3 9.6 %all-to-all-start.4 = ((f32[8,2,16,512]{3,2,1,0:T(8,128)}), f32[8,2,16,512]{3,2,1,0:T(8,128)}, u32[]{:S(2)}, u32[]{:S(2)}) async-start(f32[8,2,16,512]{3,2,1,0:T(8,128)} %broadcast_in_dim.145), calls=%async_computation.4 | async-start | bytes 1048576 | tf_op jit(solution)/shard_map/all_to_all | solution.py:146
  124.0 0.8 copy.46
  124.8 1.2 reshape.267
  126.0 19.3 %factor.2 = (f32[256,256]{1,0:T(8,128)}, f32[256,256]{1,0:T(8,128)}) custom-call(f32[256,256]{1,0:T(8,128)} %bitcast.120, f32[256,256]{1,0:T(8,128)} %bitcast.109), custom_call_target="tpu_custom_call" | custom-call | tf_op jit(solution)/shard_map/factor/pallas_call | solution.py:133
  145.3 1.1 copy.47
  146.4 1.3 convolution_add_fusion.3
  147.8 0.9 slice_add_fusion.3
  149.1 1.2 collective-permute-done.4
  150.4 0.8 broadcast_in_dim.148
  151.2 7.2 %all-to-all-start.5 = ((f32[8,64,256]{2,1,0:T(8,128)}), f32[8,64,256]{2,1,0:T(8,128)S(1)}, u32[]{:S(2)}, u32[]{:S(2)}) async-start(f32[8,64,256]{2,1,0:T(8,128)} %broadcast_in_dim.148), calls=%async_computation.5 | async-start | bytes 1048576 | tf_op jit(solution)/shard_map/all_to_all | solution.py:146
  158.5 17.8 %all-to-all-done.5 = f32[8,64,256]{2,1,0:T(8,128)S(1)} async-done(((f32[8,64,256]{2,1,0:T(8,128)}), f32[8,64,256]{2,1,0:T(8,128)S(1)}, u32[]{:S(2)}, u32[]{:S(2)}) %all-to-all-start.5) | async-done | bytes 524320 | tf_op jit(solution)/shard_map/all_to_all | solution.py:146
  176.3 1.2 broadcast_in_dim.149
  177.6 8.7 %all-to-all-start.6 = ((f32[16,80,256]{2,1,0:T(8,128)}), f32[16,80,256]{2,1,0:T(8,128)S(1)}, u32[]{:S(2)}, u32[]{:S(2)}) async-start(f32[16,80,256]{2,1,0:T(8,128)} %broadcast_in_dim.149), calls=%async_computation.6 | async-start | bytes 2621440 | tf_op jit(solution)/shard_map/all_to_all | solution.py:146
  187.0 1.3 select_bitcast_fusion.3
  189.4 1.2 fusion.95
  190.6 14.5 %all-to-all-done.6 = f32[16,80,256]{2,1,0:T(8,128)S(1)} async-done(((f32[16,80,256]{2,1,0:T(8,128)}), f32[16,80,256]{2,1,0:T(8,128)S(1)}, u32[]{:S(2)}, u32[]{:S(2)}) %all-to-all-start.6) | async-done | bytes 1310752 | tf_op jit(solution)/shard_map/all_to_all | solution.py:146
  205.9 1.1 fusion.92
  207.6 0.9 slice.164
  208.4 1.2 reshape.275
  214.0 2.0 convolution_subtract_fusion.1
  216.0 1.2 fusion.6
  218.8 3.4 all-to-all-start.7
  224.2 10.8 %all-to-all-done.7 = f32[8,16,512]{2,1,0:T(8,128)S(1)} async-done(((f32[8,16,512]{2,1,0:T(8,128)}), f32[8,16,512]{2,1,0:T(8,128)S(1)}, u32[]{:S(2)}, u32[]{:S(2)}) %all-to-all-start.7) | async-done | bytes 262176 | tf_op jit(solution)/shard_map/all_to_all | solution.py:146
  235.3 27.1 %all_to_all.61 = f32[16,96,256]{2,1,0:T(8,128)S(1)} all-to-all(f32[16,96,256]{2,1,0:T(8,128)S(1)} %pad_maximum_fusion.1), channel_id=1, replica_groups=mesh['row'=16,'col_0'=8,'col_1'=2] {'row'}, dimensions={0} | all-to-all | bytes 3145728 | tf_op jit(solution)/shard_map/all_to_all | solution.py:146
  262.3 0.9 fusion.83
  263.2 1.9 collective-permute-start.7
  265.1 4.2 %collective-permute-done.7 = f32[2,16,512]{2,1,0:T(8,128)S(1)} collective-permute-done((f32[2,16,512]{2,1,0:T(8,128)S(1)}, f32[2,16,512]{2,1,0:T(8,128)S(1)}, u32[]{:S(2)}, u32[]{:S(2)}) %collective-permute-start.7) | collective-permute-done | bytes 65568 | tf_op jit(solution)/shard_map/ppermute | solution.py:158
  269.4 0.9 broadcast_in_dim.155
  270.3 8.8 %all-to-all-start.9 = ((f32[8,2,16,512]{3,2,1,0:T(8,128)}), f32[8,2,16,512]{3,2,1,0:T(8,128)S(1)}, u32[]{:S(2)}, u32[]{:S(2)}) async-start(f32[8,2,16,512]{3,2,1,0:T(8,128)} %broadcast_in_dim.155), calls=%async_computation.9 | async-start | bytes 1048576 | tf_op jit(solution)/shard_map/all_to_all | solution.py:146
  279.1 0.8 fusion.84
  279.9 0.8 copy.52
  280.7 1.2 reshape.287
  281.9 18.9 %factor.3 = (f32[256,256]{1,0:T(8,128)}, f32[256,256]{1,0:T(8,128)}) custom-call(f32[256,256]{1,0:T(8,128)} %bitcast.121, f32[256,256]{1,0:T(8,128)} %bitcast.117), custom_call_target="tpu_custom_call" | custom-call | tf_op jit(solution)/shard_map/factor/pallas_call | solution.py:133
  300.9 1.1 copy.53
  302.0 1.2 convolution_add_fusion.2
  303.3 0.9 slice_add_fusion.1
  305.1 0.8 collective-permute-done.9
  306.6 7.2 %all-to-all-start.10 = ((f32[8,16,256]{2,1,0:T(8,128)}), f32[8,16,256]{2,1,0:T(8,128)S(1)}, u32[]{:S(2)}, u32[]{:S(2)}) async-start(f32[8,16,256]{2,1,0:T(8,128)} %broadcast_in_dim.157), calls=%async_computation.10 | async-start | bytes 262144 | tf_op jit(solution)/shard_map/all_to_all | solution.py:146
  313.9 9.5 %all-to-all-done.10 = f32[8,16,256]{2,1,0:T(8,128)S(1)} async-done(((f32[8,16,256]{2,1,0:T(8,128)}), f32[8,16,256]{2,1,0:T(8,128)S(1)}, u32[]{:S(2)}, u32[]{:S(2)}) %all-to-all-start.10) | async-done | bytes 131104 | tf_op jit(solution)/shard_map/all_to_all | solution.py:146
  323.4 1.0 broadcast_in_dim.158
  324.4 8.7 %all-to-all-start.11 = ((f32[16,48,256]{2,1,0:T(8,128)}), f32[16,48,256]{2,1,0:T(8,128)S(1)}, u32[]{:S(2)}, u32[]{:S(2)}) async-start(f32[16,48,256]{2,1,0:T(8,128)} %broadcast_in_dim.158), calls=%async_computation.11 | async-start | bytes 1572864 | tf_op jit(solution)/shard_map/all_to_all | solution.py:146
  333.1 1.2 select_bitcast_fusion.1
  334.6 0.8 copy-done.22
  336.3 8.8 %all-to-all-done.11 = f32[16,48,256]{2,1,0:T(8,128)S(1)} async-done(((f32[16,48,256]{2,1,0:T(8,128)}), f32[16,48,256]{2,1,0:T(8,128)S(1)}, u32[]{:S(2)}, u32[]{:S(2)}) %all-to-all-start.11) | async-done | bytes 786464 | tf_op jit(solution)/shard_map/all_to_all | solution.py:146
  347.9 2.7 fusion.3
  350.5 2.8 reshape.291
  (177 shorter events, 21.4 us)
Async XLA Ops:
  2.4 17.6 %all-to-all-start = ((f32[16,16,512]{2,1,0:T(8,128)}), f32[16,16,512]{2,1,0:T(8,128)S(1)}, u32[]{:S(2)}, u32[]{:S(2)}) async-start(f32[16,16,512]{2,1,0:T(8,128)} %reshape.260), calls=%async_computation | async-start | bytes 1048576 | tf_op jit(solution)/shard_map/all_to_all | solution.py:146
  20.1 21.7 %copy-start.30 = (f32[16,16,512]{2,1,0:T(8,128)}, f32[16,16,512]{2,1,0:T(8,128)S(1)}, u32[]{:S(2)}) copy-start(f32[16,16,512]{2,1,0:T(8,128)S(1)} %all-to-all-done) | copy-start | bytes 1572868
  21.1 14.0 %all-to-all-start.1 = ((f32[16,16,512]{2,1,0:T(8,128)}), f32[16,16,512]{2,1,0:T(8,128)S(1)}, u32[]{:S(2)}, u32[]{:S(2)}) async-start(f32[16,16,512]{2,1,0:T(8,128)} %broadcast_in_dim.136), calls=%async_computation.1 | async-start | bytes 1048576 | tf_op jit(solution)/shard_map/all_to_all | solution.py:146
  25.9 31.8 %copy-start.18 = (f32[2,256,2,256]{3,2,1,0:T(2,128)S(1)}, f32[2,256,2,256]{3,2,1,0:T(2,128)}, u32[]{:S(2)}) copy-start(f32[2,256,2,256]{3,2,1,0:T(2,128)} %param.1) | copy-start | bytes 3145732
  35.6 3.6 %collective-permute-start = (f32[32,256]{1,0:T(8,128)S(1)}, f32[32,256]{1,0:T(8,128)S(1)}, u32[]{:S(2)}, u32[]{:S(2)}) collective-permute-start(f32[32,256]{1,0:T(8,128)S(1)} %pad_maximum_fusion.26), channel_id=1, source_target_pairs={{0,1},{1,0},{2,3},{3,2},{4,5},{5,4},{6,7},{7,6},{8,9},{9,8},{10,11... | collective-permute-start | bytes 98312 | tf_op jit(solution)/shard_map/ppermute | solution.py:162
  35.7 5.2 %collective-permute-start.1 = (f32[16,512]{1,0:T(8,128)S(1)}, f32[16,512]{1,0:T(8,128)S(1)}, u32[]{:S(2)}, u32[]{:S(2)}) collective-permute-start(f32[16,512]{1,0:T(8,128)S(1)} %fusion.40), channel_id=1, source_target_pairs={{0,0},{1,16},{2,32},{3,48},{4,64},{5,80},{6,96},{7,112},{8,128},{9... | collective-permute-start | bytes 98312 | tf_op jit(solution)/shard_map/ppermute | solution.py:158
  41.8 33.4 %all-to-all-start.2 = ((f32[8,32,512]{2,1,0:T(8,128)}), f32[8,32,512]{2,1,0:T(8,128)S(1)}, u32[]{:S(2)}, u32[]{:S(2)}) async-start(f32[8,32,512]{2,1,0:T(8,128)} %broadcast_in_dim.138), calls=%async_computation.2 | async-start | bytes 1048576 | tf_op jit(solution)/shard_map/all_to_all | solution.py:146
  75.3 1.6 collective-permute-start.2
  77.0 0.8 copy-start.5
  106.3 6.1 %collective-permute-start.3 = (f32[2,16,512]{2,1,0:T(8,128)S(1)}, f32[2,16,512]{2,1,0:T(8,128)S(1)}, u32[]{:S(2)}, u32[]{:S(2)}) collective-permute-start(f32[2,16,512]{2,1,0:T(8,128)S(1)} %pad_maximum_fusion.21), channel_id=1, source_target_pairs={{0,0},{1,16},{2,32},{3,48},{4,64},{5,80},{6,96},{7,112},{8,128},{9... | collective-permute-start | bytes 196616 | tf_op jit(solution)/shard_map/ppermute | solution.py:158
  113.3 32.0 %all-to-all-start.4 = ((f32[8,2,16,512]{3,2,1,0:T(8,128)}), f32[8,2,16,512]{3,2,1,0:T(8,128)}, u32[]{:S(2)}, u32[]{:S(2)}) async-start(f32[8,2,16,512]{3,2,1,0:T(8,128)} %broadcast_in_dim.145), calls=%async_computation.4 | async-start | bytes 1048576 | tf_op jit(solution)/shard_map/all_to_all | solution.py:146
  124.0 23.8 %copy-start.6 = (f32[8,2,16,512]{3,2,1,0:T(8,128)S(1)}, f32[8,2,16,512]{3,2,1,0:T(8,128)}, u32[]{:S(2)}) copy-start(f32[8,2,16,512]{3,2,1,0:T(8,128)} %copy-done.5) | copy-start | bytes 1572868
  126.0 21.7 %copy-start.1 = (f32[256,512]{1,0:T(8,128)}, f32[256,512]{1,0:T(8,128)S(1)}, u32[]{:S(2)}) copy-start(f32[256,512]{1,0:T(8,128)S(1)} %reshape.267) | copy-start | bytes 1572868
  146.4 2.6 copy-start.25
  149.0 1.3 collective-permute-start.4
  151.2 25.0 %all-to-all-start.5 = ((f32[8,64,256]{2,1,0:T(8,128)}), f32[8,64,256]{2,1,0:T(8,128)S(1)}, u32[]{:S(2)}, u32[]{:S(2)}) async-start(f32[8,64,256]{2,1,0:T(8,128)} %broadcast_in_dim.148), calls=%async_computation.5 | async-start | bytes 1048576 | tf_op jit(solution)/shard_map/all_to_all | solution.py:146
  158.4 28.6 %collective-permute-start.6 = (f32[8,2,16,512]{3,2,1,0:T(8,128)}, f32[8,2,16,512]{3,2,1,0:T(8,128)}, u32[]{:S(2)}, u32[]{:S(2)}) collective-permute-start(f32[8,2,16,512]{3,2,1,0:T(8,128)} %all-to-all-done.4), channel_id=1, source_target_pairs={{0,1},{1,0},{2,3},{3,2},{4,5},{5,4},{6,7},{7,6},{8,9},{9,8},{10,11... | collective-permute-start | bytes 1572872 | tf_op jit(solution)/shard_map/ppermute | solution.py:162
  176.3 37.0 %copy-start.32 = (f32[64,256]{1,0:T(8,128)}, f32[64,256]{1,0:T(8,128)S(1)}, u32[]{:S(2)}) copy-start(f32[64,256]{1,0:T(8,128)S(1)} %reduce_sum.56) | copy-start | bytes 196612
  177.6 8.7 %copy-start.15 = (f32[256,256]{1,0:T(8,128)S(1)}, f32[256,256]{1,0:T(8,128)}, u32[]{:S(2)}) copy-start(f32[256,256]{1,0:T(8,128)} %get-tuple-element.17) | copy-start | bytes 786436
  177.6 8.7 %copy-start.17 = (f32[256,256]{0,1:T(8,128)S(1)}, f32[256,256]{0,1:T(8,128)}, u32[]{:S(2)}) copy-start(f32[256,256]{0,1:T(8,128)} %copy.46) | copy-start | bytes 786436
  177.6 27.5 %all-to-all-start.6 = ((f32[16,80,256]{2,1,0:T(8,128)}), f32[16,80,256]{2,1,0:T(8,128)S(1)}, u32[]{:S(2)}, u32[]{:S(2)}) async-start(f32[16,80,256]{2,1,0:T(8,128)} %broadcast_in_dim.149), calls=%async_computation.6 | async-start | bytes 2621440 | tf_op jit(solution)/shard_map/all_to_all | solution.py:146
  188.5 1.0 copy-start
  188.6 2.0 copy-start.3
  209.6 1.0 copy-start.13
  209.6 1.0 copy-start.29
  210.0 1.1 copy-start.2
  211.1 1.2 copy-start.19
  211.1 1.8 copy-start.31
  211.1 2.4 copy-start.8
  211.1 2.4 copy-start.9
  211.1 2.4 copy-start.21
  213.0 4.3 %collective-permute-start.5 = (f32[32,256]{1,0:T(8,128)}, f32[32,256]{1,0:T(8,128)}, u32[]{:S(2)}, u32[]{:S(2)}) collective-permute-start(f32[32,256]{1,0:T(8,128)} %pad_maximum_fusion.27), channel_id=1, source_target_pairs={{0,1},{1,0},{2,3},{3,2},{4,5},{5,4},{6,7},{7,6},{8,9},{9,8},{10,11... | collective-permute-start | bytes 98312 | tf_op jit(solution)/shard_map/ppermute | solution.py:162
  214.0 2.0 slice-start
  216.0 6.2 %copy-start.4 = (f32[16,1,16,512]{3,2,1,0:T(8,128)S(1)}, f32[16,1,16,512]{3,2,1,0:T(8,128)}, u32[]{:S(2)}) copy-start(f32[16,1,16,512]{3,2,1,0:T(8,128)} %copy-done.3) | copy-start | bytes 1572868
  216.0 6.2 %copy-start.10 = (f32[256,256]{1,0:T(8,128)S(1)}, f32[256,256]{1,0:T(8,128)}, u32[]{:S(2)}) copy-start(f32[256,256]{1,0:T(8,128)} %get-tuple-element.60) | copy-start | bytes 786436
  216.0 6.2 %copy-start.14 = (f32[256,256]{1,0:T(8,128)S(1)}, f32[256,256]{1,0:T(8,128)}, u32[]{:S(2)}) copy-start(f32[256,256]{1,0:T(8,128)} %bitcast_add_fusion) | copy-start | bytes 786436
  216.0 6.2 %copy-start.20 = (f32[256,256]{1,0:T(8,128)S(1)}, f32[256,256]{1,0:T(8,128)}, u32[]{:S(2)}) copy-start(f32[256,256]{1,0:T(8,128)} %copy-done.19) | copy-start | bytes 786436
  218.8 16.2 %all-to-all-start.7 = ((f32[8,16,512]{2,1,0:T(8,128)}), f32[8,16,512]{2,1,0:T(8,128)S(1)}, u32[]{:S(2)}, u32[]{:S(2)}) async-start(f32[8,16,512]{2,1,0:T(8,128)} %broadcast_in_dim.151), calls=%async_computation.7 | async-start | bytes 524288 | tf_op jit(solution)/shard_map/all_to_all | solution.py:146
  222.2 1.2 copy-start.11
  263.2 6.2 %collective-permute-start.7 = (f32[2,16,512]{2,1,0:T(8,128)S(1)}, f32[2,16,512]{2,1,0:T(8,128)S(1)}, u32[]{:S(2)}, u32[]{:S(2)}) collective-permute-start(f32[2,16,512]{2,1,0:T(8,128)S(1)} %pad_maximum_fusion.24), channel_id=1, source_target_pairs={{0,0},{1,16},{2,32},{3,48},{4,64},{5,80},{6,96},{7,112},{8,128},{9... | collective-permute-start | bytes 196616 | tf_op jit(solution)/shard_map/ppermute | solution.py:158
  270.3 30.6 %all-to-all-start.9 = ((f32[8,2,16,512]{3,2,1,0:T(8,128)}), f32[8,2,16,512]{3,2,1,0:T(8,128)S(1)}, u32[]{:S(2)}, u32[]{:S(2)}) async-start(f32[8,2,16,512]{3,2,1,0:T(8,128)} %broadcast_in_dim.155), calls=%async_computation.9 | async-start | bytes 1048576 | tf_op jit(solution)/shard_map/all_to_all | solution.py:146
  301.9 2.6 copy-start.27
  301.9 31.2 %collective-permute-start.8 = (f32[8,2,16,512]{3,2,1,0:T(8,128)S(1)}, f32[8,2,16,512]{3,2,1,0:T(8,128)}, u32[]{:S(2)}, u32[]{:S(2)}) collective-permute-start(f32[8,2,16,512]{3,2,1,0:T(8,128)S(1)} %all-to-all-done.9), channel_id=1, source_target_pairs={{0,1},{1,0},{2,3},{3,2},{4,5},{5,4},{6,7},{7,6},{8,9},{9,8},{10,11... | collective-permute-start | bytes 1572872 | tf_op jit(solution)/shard_map/ppermute | solution.py:162
  304.5 1.4 collective-permute-start.9
  306.6 16.8 %all-to-all-start.10 = ((f32[8,16,256]{2,1,0:T(8,128)}), f32[8,16,256]{2,1,0:T(8,128)S(1)}, u32[]{:S(2)}, u32[]{:S(2)}) async-start(f32[8,16,256]{2,1,0:T(8,128)} %broadcast_in_dim.157), calls=%async_computation.10 | async-start | bytes 262144 | tf_op jit(solution)/shard_map/all_to_all | solution.py:146
  324.4 20.7 %all-to-all-start.11 = ((f32[16,48,256]{2,1,0:T(8,128)}), f32[16,48,256]{2,1,0:T(8,128)S(1)}, u32[]{:S(2)}, u32[]{:S(2)}) async-start(f32[16,48,256]{2,1,0:T(8,128)} %broadcast_in_dim.158), calls=%async_computation.11 | async-start | bytes 1572864 | tf_op jit(solution)/shard_map/all_to_all | solution.py:146
  334.5 1.0 copy-start.22
  334.5 1.4 copy-start.7
  345.7 1.1 copy-start.23
  345.7 1.1 copy-start.24
  346.4 1.3 copy-start.12
  346.4 1.3 copy-start.16
  346.4 1.4 copy-start.26
  346.4 1.4 copy-start.28
where the time goes:
time: 359 us; the launch traced here: 354 us
  waiting for transfers between devices  111 us (31%)
  starting transfers between devices  90 us (25%)
  blocking collectives  53.7 us (15%)
  Pallas kernels  38.2 us (11%)
  local copies, waits for them, and re-layouts  28.7 us (8%)
  matrix products  20.5 us (6%)
  other arithmetic  9.79 us (3%)
    all_to_all x10, waiting for transfers between devices, exchange(): return lax.all_to_all(value, axis, 0, 0, tiled=True)  98.2 us
    all_to_all x10, starting transfers between devices, exchange(): return lax.all_to_all(value, axis, 0, 0, tiled=True)  81.8 us
    all_to_all x2, blocking collectives, exchange(): return lax.all_to_all(value, axis, 0, 0, tiled=True)  53.7 us
    pallas_call x2, Pallas kernels, factor(): pl.pallas_call(functools.partial(factor_kernel, b=32), out_shape=(square,...  38.2 us
    dot_general x31, matrix products, product(): lax.dot_general(left, right, (dims, ((), ())), precision=precision, prefe...  20.5 us
    ppermute x3, waiting for transfers between devices, transposed(): return lax.ppermute(value, ('row', *COL), pairs)  10.1 us
    broadcast_in_dim x9, local copies, waits for them, and re-layouts, copied(): copies = jnp.broadcast_to(value, (lax.axis_size(axis), *value.shape))  7.98 us
    ppermute x3, starting transfers between devices, transposed(): return lax.ppermute(value, ('row', *COL), pairs)  7.33 us
  transfers between devices with their start and end apart: 20, of which 14 were waited for; matrix products, arithmetic and copies ran while one was open for 7% of the time, Pallas kernels for 11%

commit v1 on v0

--- a/solution.py
+++ b/solution.py
@@ -198,23 +198,19 @@
         start = (panel + 1) * width
         last = panel + 1 == PANELS
         below_cols = global_cols[None, :] >= start
-        gathered = []
         if panel == 0:
             x_own, c_own, *later = [
                 jnp.where(below_cols, sent[source], 0.0) for source in range(PANELS + 1)
             ]
-            gathered = [transposed(x_own)]
-            x_cols = copied(x_own, "row").reshape(width, local)
-        x_piece = lax.dynamic_slice_in_dim(x_cols, own, part, 0)
-        gram_part = product(x_piece, x_cols, NT, highest)
-        top_part = jnp.where(col_index == panel + 1, x_piece[:, :width], 0.0)
-        summed = core_sum(jnp.concatenate([gram_part, top_part]))
-        lines = copied(jnp.concatenate([summed.reshape(part, local), *gathered]), COL[0])
-        sums = jnp.sum(lines[:, :part], axis=0).reshape(2 * part, width)
+            x_rows = both_cores(copied(transposed(x_own), COL[0])).reshape(width, local)
+        u_part = product(x_rows, dense)
+        x_piece = lax.dynamic_slice_in_dim(x_rows, col_index * part, part, 0)
+        gram_part = product(x_piece, x_rows, NT, highest)
+        top_part = jnp.where(row_index == panel + 1, x_piece[:, :width], 0.0)
+        shared = [gram_part, top_part, c_own.reshape(2 * part, width)]
         if panel == 0:
-            x_rows = both_cores(lines[:, part:]).reshape(width, local)
-        u_part = product(x_rows, dense)
-        shared = jnp.concatenate([sums, c_own.reshape(2 * part, width)])
+            shared.append(x_own.reshape(2 * part, width))
+        shared = jnp.concatenate(shared)
         merged = jnp.concatenate(
             [
                 jnp.broadcast_to(shared, (devices, *shared.shape)),
@@ -223,10 +219,13 @@
             axis=1,
         )
         merged = exchange(merged, "row")
-        gram = merged[:, :part].reshape(width, width)
-        top = merged[:, part : 2 * part].reshape(width, width).T
+        sums = copied(jnp.sum(merged[:, : 2 * part], axis=0), COL)
+        gram = sums[:, :part].reshape(width, width)
+        top = sums[:, part:].reshape(width, width).T
         c_cols = merged[:, 2 * part : 4 * part].reshape(width, local)
-        u_own = jnp.sum(merged[:, 4 * part :], axis=0).reshape(part, local)
+        if panel == 0:
+            x_cols = merged[:, 4 * part : 6 * part].reshape(width, local)
+        u_own = jnp.sum(merged[:, -2 * part :], axis=0).reshape(part, local)
         u_own = jnp.where(below_cols, u_own, 0.0)
         pair = transposed(jnp.stack([u_own, c_own]))
         pair = copied(pair, COL[0])
@@ -251,7 +250,10 @@
                 jnp.where(col_index == panel + 2, w_own[:, :width], 0.0),
                 jnp.where(col_index == panel + 2, across, 0.0),
             ]
-        sums = jnp.sum(copied(core_sum(jnp.concatenate(parts)), COL[0]), axis=0)
+        if last:
+            sums = jnp.sum(copied(parts[0], COL), axis=0)
+        else:
+            sums = jnp.sum(copied(core_sum(jnp.concatenate(parts)), COL[0]), axis=0)
         shared = jnp.concatenate([w_own.reshape(2 * part, width), sums[: 3 * part]])
         shared = copied(shared, "row")
         w_cols = shared[:, : 2 * part].reshape(width, local)

time: 359 us -> 382 us (1.064)
  blocking collectives: 53.7 us -> 88.5 us
  starting transfers between devices: 90 us -> 71 us
    all_to_all x2 -> x3, blocking collectives: 53.7 us -> 88.5 us  [exchange(): return lax.all_to_all(value, axis, 0, 0, tiled=True)]
    all_to_all x10 -> x9, starting transfers between devices: 81.8 us -> 62 us  [exchange(): return lax.all_to_all(value, axis, 0, 0, tiled=True)]
    ppermute x3, waiting for transfers between devices: 10.1 us -> 23.2 us  [transposed(): return lax.ppermute(value, ('row', *COL), pairs)]
    all_to_all x10 -> x9, waiting for transfers between devices: 98.2 us -> 86.1 us  [exchange(): return lax.all_to_all(value, axis, 0, 0, tiled=True)]
  transfers between devices with their start and end apart: 20 -> 16, of which waited for: 14 -> 12; matrix products, arithmetic and copies ran while one was open for 7% -> 5% of each run, Pallas kernels for 11% -> 10%
where the time goes in v1:
time: 382 us; the launch traced here: 374 us
  waiting for transfers between devices  112 us (29%)
  blocking collectives  88.5 us (23%)
  starting transfers between devices  71 us (19%)
  Pallas kernels  38 us (10%)
  local copies, waits for them, and re-layouts  32.2 us (8%)
  matrix products  22.2 us (6%)
  other arithmetic  9.02 us (2%)
    all_to_all x3, blocking collectives, exchange(): return lax.all_to_all(value, axis, 0, 0, tiled=True)  88.5 us
    all_to_all x9, waiting for transfers between devices, exchange(): return lax.all_to_all(value, axis, 0, 0, tiled=True)  86.1 us
    all_to_all x9, starting transfers between devices, exchange(): return lax.all_to_all(value, axis, 0, 0, tiled=True)  62 us
    pallas_call x2, Pallas kernels, factor(): pl.pallas_call(functools.partial(factor_kernel, b=32), out_shape=(square,...  38 us
    ppermute x3, waiting for transfers between devices, transposed(): return lax.ppermute(value, ('row', *COL), pairs)  23.2 us
    dot_general x31, matrix products, product(): lax.dot_general(left, right, (dims, ((), ())), precision=precision, prefe...  22.2 us
    ppermute x3, starting transfers between devices, transposed(): return lax.ppermute(value, ('row', *COL), pairs)  8.44 us
  transfers between devices with their start and end apart: 16, of which 12 were waited for; matrix products, arithmetic and copies ran while one was open for 5% of the time, Pallas kernels for 10%

profile of v1, /device:TPU:2, one launch (start us, length us, event | category | flops | bytes accessed | tf_op | source)
XLA Modules:
  0.0 374.2 jit_solution(12430175647685870274)
XLA Ops:
  0.0 1.2 slice.116
  1.2 1.2 reshape.253
  2.4 7.6 %all-to-all-start = ((f32[16,16,512]{2,1,0:T(8,128)}), f32[16,16,512]{2,1,0:T(8,128)S(1)}, u32[]{:S(2)}, u32[]{:S(2)}) async-start(f32[16,16,512]{2,1,0:T(8,128)} %reshape.253), calls=%async_computation | async-start | bytes 1048576 | tf_op jit(solution)/shard_map/all_to_all | solution.py:146
  10.1 10.2 %all-to-all-done = f32[16,16,512]{2,1,0:T(8,128)S(1)} async-done(((f32[16,16,512]{2,1,0:T(8,128)}), f32[16,16,512]{2,1,0:T(8,128)S(1)}, u32[]{:S(2)}, u32[]{:S(2)}) %all-to-all-start) | async-done | bytes 524320 | tf_op jit(solution)/shard_map/all_to_all | solution.py:146
  21.1 1.9 collective-permute-start
  23.1 18.6 %collective-permute-done = f32[16,512]{0,1:T(8,128)S(1)} collective-permute-done((f32[16,512]{0,1:T(8,128)S(1)}, f32[16,512]{0,1:T(8,128)S(1)}, u32[]{:S(2)}, u32[]{:S(2)}) %collective-permute-start) | collective-permute-done | bytes 32800 | tf_op jit(solution)/shard_map/ppermute | solution.py:158
  41.8 29.0 %all_to_all.60 = f32[8,16,512]{2,1,0:T(8,128)S(1)} all-to-all(f32[8,16,512]{2,1,0:T(8,128)S(1)} %broadcast_in_dim.137), channel_id=1, replica_groups=mesh['row'=16,'col_0'=8,'col_1'=2] {'col_0'}, dimensions={0} | all-to-all | bytes 524288 | tf_op jit(solution)/shard_map/all_to_all | solution.py:146
  71.1 1.3 collective-permute-done.1
  74.1 32.5 %all_to_all.61 = f32[16,128,256]{2,1,0:T(8,128)S(1)} all-to-all(f32[16,128,256]{2,1,0:T(8,128)S(1)} %pad_maximum_fusion), channel_id=1, replica_groups=mesh['row'=16,'col_0'=8,'col_1'=2] {'row'}, dimensions={0} | all-to-all | bytes 4194304 | tf_op jit(solution)/shard_map/all_to_all | solution.py:146
  106.8 0.8 broadcast_in_dim.145
  107.6 3.6 all-to-all-start.4
  111.2 3.3 collective-permute-start.2
  114.5 2.3 collective-permute-done.2
  116.8 11.0 %all-to-all-done.4 = f32[16,32,256]{2,1,0:T(8,128)S(1)} async-done(((f32[16,32,256]{2,1,0:T(8,128)}), f32[16,32,256]{2,1,0:T(8,128)S(1)}, u32[]{:S(2)}, u32[]{:S(2)}) %all-to-all-start.4) | async-done | bytes 524320 | tf_op jit(solution)/shard_map/all_to_all | solution.py:146
  127.8 0.9 broadcast_in_dim.144
  128.7 5.5 %all-to-all-start.3 = ((f32[8,2,16,512]{3,2,1,0:T(8,128)}), f32[8,2,16,512]{3,2,1,0:T(8,128)}, u32[]{:S(2)}, u32[]{:S(2)}) async-start(f32[8,2,16,512]{3,2,1,0:T(8,128)} %broadcast_in_dim.144), calls=%async_computation.3 | async-start | bytes 1048576 | tf_op jit(solution)/shard_map/all_to_all | solution.py:146
  135.6 1.8 fusion.83
  137.4 0.8 copy.107
  138.2 19.1 %factor.2 = (f32[256,256]{1,0:T(8,128)}, f32[256,256]{1,0:T(8,128)}) custom-call(f32[256,256]{1,0:T(8,128)} %bitcast.114, f32[256,256]{1,0:T(8,128)} %bitcast.102), custom_call_target="tpu_custom_call" | custom-call | tf_op jit(solution)/shard_map/factor/pallas_call | solution.py:133
  157.3 1.1 copy.112
  158.5 1.9 slice_add_fusion.3
  160.5 1.6 convolution_add_fusion.3
  162.8 1.3 collective-permute-done.4
  164.2 0.8 broadcast_in_dim.148
  165.1 7.2 %all-to-all-start.5 = ((f32[8,64,256]{2,1,0:T(8,128)}), f32[8,64,256]{2,1,0:T(8,128)}, u32[]{:S(2)}, u32[]{:S(2)}) async-start(f32[8,64,256]{2,1,0:T(8,128)} %broadcast_in_dim.148), calls=%async_computation.5 | async-start | bytes 1048576 | tf_op jit(solution)/shard_map/all_to_all | solution.py:146
  173.3 16.9 %all-to-all-done.5 = f32[8,64,256]{2,1,0:T(8,128)} async-done(((f32[8,64,256]{2,1,0:T(8,128)}), f32[8,64,256]{2,1,0:T(8,128)}, u32[]{:S(2)}, u32[]{:S(2)}) %all-to-all-start.5) | async-done | bytes 524320 | tf_op jit(solution)/shard_map/all_to_all | solution.py:146
  190.2 1.1 reduce_sum.56
  191.3 1.2 broadcast_in_dim.149
  192.5 11.1 %all-to-all-start.6 = ((f32[16,80,256]{2,1,0:T(8,128)}), f32[16,80,256]{2,1,0:T(8,128)}, u32[]{:S(2)}, u32[]{:S(2)}) async-start(f32[16,80,256]{2,1,0:T(8,128)} %broadcast_in_dim.149), calls=%async_computation.6 | async-start | bytes 2621440 | tf_op jit(solution)/shard_map/all_to_all | solution.py:146
  204.4 1.3 select_bitcast_fusion.3
  205.9 0.8 copy-done.9
  207.2 1.2 fusion.87
  208.4 14.2 %all-to-all-done.6 = f32[16,80,256]{2,1,0:T(8,128)} async-done(((f32[16,80,256]{2,1,0:T(8,128)}), f32[16,80,256]{2,1,0:T(8,128)}, u32[]{:S(2)}, u32[]{:S(2)}) %all-to-all-start.6) | async-done | bytes 1310752 | tf_op jit(solution)/shard_map/all_to_all | solution.py:146
  222.6 2.0 fusion.78
  225.2 1.9 slice.175
  227.1 2.0 reshape.268
  229.1 1.5 fusion.88
  230.6 1.4 fusion.85
  233.5 1.1 convolution_subtract_fusion.1
  236.2 1.4 fusion.89
  237.7 1.1 reshape.270
  238.8 2.0 fusion.6
  241.2 26.9 %all_to_all.62 = f32[16,96,256]{2,1,0:T(8,128)S(1)} all-to-all(f32[16,96,256]{2,1,0:T(8,128)S(1)} %pad_maximum_fusion.1), channel_id=1, replica_groups=mesh['row'=16,'col_0'=8,'col_1'=2] {'row'}, dimensions={0} | all-to-all | bytes 3145728 | tf_op jit(solution)/shard_map/all_to_all | solution.py:146
  268.2 0.9 slice_reduce_fusion
  269.0 0.9 broadcast_in_dim.154
  269.9 3.7 all-to-all-start.9
  273.8 3.3 collective-permute-start.5
  277.0 2.3 collective-permute-done.5
  279.4 10.9 %all-to-all-done.9 = f32[16,32,256]{2,1,0:T(8,128)S(1)} async-done(((f32[16,32,256]{2,1,0:T(8,128)}), f32[16,32,256]{2,1,0:T(8,128)S(1)}, u32[]{:S(2)}, u32[]{:S(2)}) %all-to-all-start.9) | async-done | bytes 524320 | tf_op jit(solution)/shard_map/all_to_all | solution.py:146
  290.2 0.9 broadcast_in_dim.153
  291.2 5.5 %all-to-all-start.8 = ((f32[8,2,16,512]{3,2,1,0:T(8,128)}), f32[8,2,16,512]{3,2,1,0:T(8,128)S(1)}, u32[]{:S(2)}, u32[]{:S(2)}) async-start(f32[8,2,16,512]{3,2,1,0:T(8,128)} %broadcast_in_dim.153), calls=%async_computation.8 | async-start | bytes 1048576 | tf_op jit(solution)/shard_map/all_to_all | solution.py:146
  296.8 1.4 fusion.5
  298.2 1.3 reshape.276
  300.3 0.8 copy.123
  301.2 18.9 %factor.3 = (f32[256,256]{1,0:T(8,128)}, f32[256,256]{1,0:T(8,128)}) custom-call(f32[256,256]{1,0:T(8,128)} %bitcast.115, f32[256,256]{1,0:T(8,128)} %bitcast.112), custom_call_target="tpu_custom_call" | custom-call | tf_op jit(solution)/shard_map/factor/pallas_call | solution.py:133
  320.1 1.1 copy.124
  321.2 0.9 slice_add_fusion.1
  323.9 7.3 %all-to-all-start.10 = ((f32[16,16,256]{2,1,0:T(8,128)}), f32[16,16,256]{2,1,0:T(8,128)S(1)}, u32[]{:S(2)}, u32[]{:S(2)}) async-start(f32[16,16,256]{2,1,0:T(8,128)} %broadcast_in_dim.157), calls=%async_computation.10 | async-start | bytes 524288 | tf_op jit(solution)/shard_map/all_to_all | solution.py:146
  331.8 10.6 %all-to-all-done.10 = f32[16,16,256]{2,1,0:T(8,128)S(1)} async-done(((f32[16,16,256]{2,1,0:T(8,128)}), f32[16,16,256]{2,1,0:T(8,128)S(1)}, u32[]{:S(2)}, u32[]{:S(2)}) %all-to-all-start.10) | async-done | bytes 262176 | tf_op jit(solution)/shard_map/all_to_all | solution.py:146
  342.4 1.0 broadcast_in_dim.158
  343.4 10.4 %all-to-all-start.11 = ((f32[16,48,256]{2,1,0:T(8,128)}), f32[16,48,256]{2,1,0:T(8,128)S(1)}, u32[]{:S(2)}, u32[]{:S(2)}) async-start(f32[16,48,256]{2,1,0:T(8,128)} %broadcast_in_dim.158), calls=%async_computation.11 | async-start | bytes 1572864 | tf_op jit(solution)/shard_map/all_to_all | solution.py:146
  355.5 12.4 %all-to-all-done.11 = f32[16,48,256]{2,1,0:T(8,128)S(1)} async-done(((f32[16,48,256]{2,1,0:T(8,128)}), f32[16,48,256]{2,1,0:T(8,128)S(1)}, u32[]{:S(2)}, u32[]{:S(2)}) %all-to-all-start.11) | async-done | bytes 786464 | tf_op jit(solution)/shard_map/all_to_all | solution.py:146
  370.7 1.7 fusion.3
  372.4 1.6 reshape.280
  (166 shorter events, 18.9 us)
Async XLA Ops:
  2.4 68.4 %copy-start.13 = (f32[2,256,2,256]{3,2,1,0:T(2,128)S(1)}, f32[2,256,2,256]{3,2,1,0:T(2,128)}, u32[]{:S(2)}) copy-start(f32[2,256,2,256]{3,2,1,0:T(2,128)} %param.1) | copy-start | bytes 3145732
  2.4 17.8 %all-to-all-start = ((f32[16,16,512]{2,1,0:T(8,128)}), f32[16,16,512]{2,1,0:T(8,128)S(1)}, u32[]{:S(2)}, u32[]{:S(2)}) async-start(f32[16,16,512]{2,1,0:T(8,128)} %reshape.253), calls=%async_computation | async-start | bytes 1048576 | tf_op jit(solution)/shard_map/all_to_all | solution.py:146
  21.1 20.5 %collective-permute-start = (f32[16,512]{0,1:T(8,128)S(1)}, f32[16,512]{0,1:T(8,128)S(1)}, u32[]{:S(2)}, u32[]{:S(2)}) collective-permute-start(f32[16,512]{0,1:T(8,128)S(1)} %bitcast_select_fusion.1), channel_id=1, source_target_pairs={{0,0},{1,16},{2,32},{3,48},{4,64},{5,80},{6,96},{7,112},{8,128},{9... | collective-permute-start | bytes 98312 | tf_op jit(solution)/shard_map/ppermute | solution.py:158
  70.8 1.5 collective-permute-start.1
  107.6 20.2 %all-to-all-start.4 = ((f32[16,32,256]{2,1,0:T(8,128)}), f32[16,32,256]{2,1,0:T(8,128)S(1)}, u32[]{:S(2)}, u32[]{:S(2)}) async-start(f32[16,32,256]{2,1,0:T(8,128)} %broadcast_in_dim.145), calls=%async_computation.4 | async-start | bytes 1048576 | tf_op jit(solution)/shard_map/all_to_all | solution.py:146
  111.2 5.6 %collective-permute-start.2 = (f32[2,16,512]{2,1,0:T(8,128)S(1)}, f32[2,16,512]{2,1,0:T(8,128)S(1)}, u32[]{:S(2)}, u32[]{:S(2)}) collective-permute-start(f32[2,16,512]{2,1,0:T(8,128)S(1)} %pad_maximum_fusion.21), channel_id=1, source_target_pairs={{0,0},{1,16},{2,32},{3,48},{4,64},{5,80},{6,96},{7,112},{8,128},{9... | collective-permute-start | bytes 196616 | tf_op jit(solution)/shard_map/ppermute | solution.py:158
  127.8 6.5 %copy-start.17 = (f32[16,32,256]{2,1,0:T(8,128)}, f32[16,32,256]{2,1,0:T(8,128)S(1)}, u32[]{:S(2)}) copy-start(f32[16,32,256]{2,1,0:T(8,128)S(1)} %all-to-all-done.4) | copy-start | bytes 1572868
  128.7 28.6 %all-to-all-start.3 = ((f32[8,2,16,512]{3,2,1,0:T(8,128)}), f32[8,2,16,512]{3,2,1,0:T(8,128)}, u32[]{:S(2)}, u32[]{:S(2)}) async-start(f32[8,2,16,512]{3,2,1,0:T(8,128)} %broadcast_in_dim.144), calls=%async_computation.3 | async-start | bytes 1048576 | tf_op jit(solution)/shard_map/all_to_all | solution.py:146
  134.5 3.7 %copy-start.11 = (f32[256,512]{1,0:T(8,128)}, f32[256,512]{1,0:T(8,128)S(1)}, u32[]{:S(2)}) copy-start(f32[256,512]{1,0:T(8,128)S(1)} %reshape.264) | copy-start | bytes 1572868
  157.3 3.1 copy-start.8
  158.5 3.6 copy-start.25
  162.5 9.8 %copy-start.31 = (f32[1,16,512]{2,1,0:T(8,128)S(1)}, f32[1,16,512]{2,1,0:T(8,128)}, u32[]{:S(2)}) copy-start(f32[1,16,512]{2,1,0:T(8,128)} %get-tuple-element.49) | copy-start | bytes 98308
  162.7 1.4 collective-permute-start.4
  165.1 25.1 %all-to-all-start.5 = ((f32[8,64,256]{2,1,0:T(8,128)}), f32[8,64,256]{2,1,0:T(8,128)}, u32[]{:S(2)}, u32[]{:S(2)}) async-start(f32[8,64,256]{2,1,0:T(8,128)} %broadcast_in_dim.148), calls=%async_computation.5 | async-start | bytes 1048576 | tf_op jit(solution)/shard_map/all_to_all | solution.py:146
  172.3 32.1 %collective-permute-start.3 = (f32[8,2,16,512]{3,2,1,0:T(8,128)}, f32[8,2,16,512]{3,2,1,0:T(8,128)}, u32[]{:S(2)}, u32[]{:S(2)}) collective-permute-start(f32[8,2,16,512]{3,2,1,0:T(8,128)} %all-to-all-done.3), channel_id=1, source_target_pairs={{0,1},{1,0},{2,3},{3,2},{4,5},{5,4},{6,7},{7,6},{8,9},{9,8},{10,11... | collective-permute-start | bytes 1572872 | tf_op jit(solution)/shard_map/ppermute | solution.py:162
  191.3 41.5 %copy-start.30 = (f32[64,256]{1,0:T(8,128)}, f32[64,256]{1,0:T(8,128)S(1)}, u32[]{:S(2)}) copy-start(f32[64,256]{1,0:T(8,128)S(1)} %reduce_sum.56) | copy-start | bytes 196612
  192.5 11.1 %copy-start.12 = (f32[256,256]{0,1:T(8,128)S(1)}, f32[256,256]{0,1:T(8,128)}, u32[]{:S(2)}) copy-start(f32[256,256]{0,1:T(8,128)} %copy.107) | copy-start | bytes 786436
  192.5 30.1 %all-to-all-start.6 = ((f32[16,80,256]{2,1,0:T(8,128)}), f32[16,80,256]{2,1,0:T(8,128)}, u32[]{:S(2)}, u32[]{:S(2)}) async-start(f32[16,80,256]{2,1,0:T(8,128)} %broadcast_in_dim.149), calls=%async_computation.6 | async-start | bytes 2621440 | tf_op jit(solution)/shard_map/all_to_all | solution.py:146
  205.8 1.0 copy-start.9
  205.8 1.4 copy-start
  229.1 2.9 copy-start.29
  230.6 2.4 copy-start.4
  230.6 2.4 copy-start.16
  232.8 1.8 copy-start.1
  233.5 1.2 copy-start.7
  234.6 1.6 copy-start.5
  235.0 1.2 copy-start.14
  236.2 2.6 copy-start.2
  236.2 2.6 slice-start
  269.9 26.8 %copy-start.15 = (f32[256,256]{1,0:T(8,128)S(1)}, f32[256,256]{1,0:T(8,128)}, u32[]{:S(2)}) copy-start(f32[256,256]{1,0:T(8,128)} %copy-done.14) | copy-start | bytes 786436
  269.9 20.3 %all-to-all-start.9 = ((f32[16,32,256]{2,1,0:T(8,128)}), f32[16,32,256]{2,1,0:T(8,128)S(1)}, u32[]{:S(2)}, u32[]{:S(2)}) async-start(f32[16,32,256]{2,1,0:T(8,128)} %broadcast_in_dim.154), calls=%async_computation.9 | async-start | bytes 1048576 | tf_op jit(solution)/shard_map/all_to_all | solution.py:146
  273.8 5.6 %collective-permute-start.5 = (f32[2,16,512]{2,1,0:T(8,128)S(1)}, f32[2,16,512]{2,1,0:T(8,128)S(1)}, u32[]{:S(2)}, u32[]{:S(2)}) collective-permute-start(f32[2,16,512]{2,1,0:T(8,128)S(1)} %pad_maximum_fusion.23), channel_id=1, source_target_pairs={{0,0},{1,16},{2,32},{3,48},{4,64},{5,80},{6,96},{7,112},{8,128},{9... | collective-permute-start | bytes 196616 | tf_op jit(solution)/shard_map/ppermute | solution.py:158
  290.2 1.0 copy-start.18
  291.2 28.9 %all-to-all-start.8 = ((f32[8,2,16,512]{3,2,1,0:T(8,128)}), f32[8,2,16,512]{3,2,1,0:T(8,128)S(1)}, u32[]{:S(2)}, u32[]{:S(2)}) async-start(f32[8,2,16,512]{3,2,1,0:T(8,128)} %broadcast_in_dim.153), calls=%async_computation.8 | async-start | bytes 1048576 | tf_op jit(solution)/shard_map/all_to_all | solution.py:146
  298.2 1.4 copy-start.19
  299.4 21.8 %copy-start.20 = (f32[256,512]{1,0:T(8,128)S(1)}, f32[256,512]{1,0:T(8,128)}, u32[]{:S(2)}) copy-start(f32[256,512]{1,0:T(8,128)} %fusion.5) | copy-start | bytes 1572868
  320.1 2.1 copy-start.21
  321.2 1.6 copy-start.27
  323.9 18.5 %all-to-all-start.10 = ((f32[16,16,256]{2,1,0:T(8,128)}), f32[16,16,256]{2,1,0:T(8,128)S(1)}, u32[]{:S(2)}, u32[]{:S(2)}) async-start(f32[16,16,256]{2,1,0:T(8,128)} %broadcast_in_dim.157), calls=%async_computation.10 | async-start | bytes 524288 | tf_op jit(solution)/shard_map/all_to_all | solution.py:146
  331.2 22.6 %collective-permute-start.6 = (f32[8,2,16,512]{3,2,1,0:T(8,128)S(1)}, f32[8,2,16,512]{3,2,1,0:T(8,128)S(1)}, u32[]{:S(2)}, u32[]{:S(2)}) collective-permute-start(f32[8,2,16,512]{3,2,1,0:T(8,128)S(1)} %all-to-all-done.8), channel_id=1, source_target_pairs={{0,1},{1,0},{2,3},{3,2},{4,5},{5,4},{6,7},{7,6},{8,9},{9,8},{10,11... | collective-permute-start | bytes 1572872 | tf_op jit(solution)/shard_map/ppermute | solution.py:162
  343.4 24.5 %all-to-all-start.11 = ((f32[16,48,256]{2,1,0:T(8,128)}), f32[16,48,256]{2,1,0:T(8,128)S(1)}, u32[]{:S(2)}, u32[]{:S(2)}) async-start(f32[16,48,256]{2,1,0:T(8,128)} %broadcast_in_dim.158), calls=%async_computation.11 | async-start | bytes 1572864 | tf_op jit(solution)/shard_map/all_to_all | solution.py:146
  354.1 1.0 copy-start.3
  368.8 1.0 copy-start.23
  368.8 1.0 copy-start.24
  369.2 1.3 copy-start.6
  369.2 1.3 copy-start.10
  369.2 1.4 copy-start.22
  369.2 1.4 copy-start.26
  369.2 1.5 copy-start.28

commit v2 on v1

--- a/solution.py
+++ b/solution.py
@@ -4,6 +4,7 @@
 import jax.numpy as jnp
 from jax import lax
 from jax.experimental import pallas as pl
+from jax.experimental.layout import Layout, with_layout_constraint
 from jax.experimental.pallas import tpu as pltpu
 from jax.sharding import Mesh
 from jax.sharding import PartitionSpec as P
@@ -74,15 +75,18 @@
         return (jnp.concatenate(self.low, axis=0) * jnp.sqrt(inv))[:, : self.b]
 
 
-def factor_kernel(g_ref, x_ref, r_ref, t_ref, aa, xb, wb, *, b):
+def factor_kernel(pieces_ref, r_ref, l_ref, t_ref, aa, xb, wb, *, b):
     exact = functools.partial(product, precision=highest)
-    n = g_ref.shape[0]
+    n = r_ref.shape[0]
+    part = pieces_ref.shape[1] // 2
     count = n // b
     rows = lax.broadcasted_iota(jnp.int32, (n, n), 0)
     cols = lax.broadcasted_iota(jnp.int32, (n, n), 1)
-    aa[:, :n] = g_ref[...]
+    for i in range(n // part):
+        aa[part * i : part * i + part, :n] = pieces_ref[i, :part, :]
+        xb[part * i : part * i + part, n:] = pieces_ref[i, part:, :]
     aa[:, n:] = (rows == cols).astype(jnp.float32)
-    xb[:, :n] = x_ref[...]
+    xb[:, :n] = xb[:, n:].T
     xb[:, n:] = jnp.zeros((n, n), jnp.float32)
     wb[...] = jnp.zeros((128, 2 * n), jnp.float32)
     lane = lax.broadcasted_iota(jnp.int32, (n, 128), 1)
@@ -124,22 +128,23 @@
         if k < count:
             pivot_row = xb[lo:hi, :] + upper
             pivot = pivot_row[:, win : win + 128]
+    l_ref[...] = r_ref[...].T
     t_ref[...] = xb[:, n:]
 
 
-def factor(gram, top):
-    n = gram.shape[0]
+def factor(pieces):
+    n = pieces.shape[-1]
     square = jax.ShapeDtypeStruct((n, n), jnp.float32)
     return pl.pallas_call(
         functools.partial(factor_kernel, b=32),
-        out_shape=(square, square),
+        out_shape=(square, square, square),
         scratch_shapes=[
             pltpu.VMEM((n, 2 * n), jnp.float32),
             pltpu.VMEM((n, 2 * n), jnp.float32),
             pltpu.VMEM((128, 2 * n), jnp.float32),
         ],
         name="factor",
-    )(gram, top)
+    )(pieces)
 
 
 def exchange(value, axis):
@@ -149,13 +154,17 @@
 def copied(value, axis):
     copies = jnp.broadcast_to(value, (lax.axis_size(axis), *value.shape))
     return exchange(copies, axis)
+
+
+def row_major(value):
+    return with_layout_constraint(value, Layout(major_to_minor=tuple(range(value.ndim))))
 
 
 def transposed(value):
     rows = lax.axis_size("row")
     cols = lax.axis_size(COL)
     pairs = [(r * cols + c, c * rows + r) for r in range(rows) for c in range(cols)]
-    return lax.ppermute(value, ("row", *COL), pairs)
+    return lax.ppermute(row_major(value), ("row", *COL), pairs)
 
 
 def swapped(value):
@@ -220,8 +229,7 @@
         )
         merged = exchange(merged, "row")
         sums = copied(jnp.sum(merged[:, : 2 * part], axis=0), COL)
-        gram = sums[:, :part].reshape(width, width)
-        top = sums[:, part:].reshape(width, width).T
+        pieces = sums
         c_cols = merged[:, 2 * part : 4 * part].reshape(width, local)
         if panel == 0:
             x_cols = merged[:, 4 * part : 6 * part].reshape(width, local)
@@ -229,10 +237,9 @@
         u_own = jnp.where(below_cols, u_own, 0.0)
         pair = transposed(jnp.stack([u_own, c_own]))
         pair = copied(pair, COL[0])
-        upper, core = factor(gram, top)
-        pair, upper, core = lax.optimization_barrier((pair, upper, core))
+        factors = factor(pieces)
+        pair, (upper, lower, core) = lax.optimization_barrier((pair, factors))
         u_rows, c_rows = join(both_cores(pair))
-        lower = upper.T
 
         def with_top(x, index):
             head = jnp.where(index == panel + 1, lower, 0.0)
@@ -244,7 +251,7 @@
         w_rows = u_rows + product(lower, c_rows)
         parts = [product(w_own, v_cols, NT)]
         if not last:
-            across = lax.dynamic_slice_in_dim(x_cols, own, part, 1).T
+            across = lax.dynamic_slice_in_dim(x_cols[:, :width].T, own, part, 0)
             parts += [
                 jnp.where(col_index == panel + 1, w_own[:, :width], 0.0),
                 jnp.where(col_index == panel + 2, w_own[:, :width], 0.0),
@@ -253,7 +260,7 @@
         if last:
             sums = jnp.sum(copied(parts[0], COL), axis=0)
         else:
-            sums = jnp.sum(copied(core_sum(jnp.concatenate(parts)), COL[0]), axis=0)
+            sums = jnp.sum(copied(core_sum(row_major(jnp.concatenate(parts))), COL[0]), axis=0)
         shared = jnp.concatenate([w_own.reshape(2 * part, width), sums[: 3 * part]])
         shared = copied(shared, "row")
         w_cols = shared[:, : 2 * part].reshape(width, local)
@@ -268,18 +275,23 @@
         if last:
             break
 
-        def reduced(old, w_t, v, v_others, y_others):
-            y = product(w_t, core, ((0,), (1,))) - product(v, middle, NT)
+        def y_of(w_t, v):
+            return product(w_t, core, ((0,), (1,))) - product(v, middle, NT)
+
+        def reduced(old, y, v, v_others, y_others):
             both = jnp.concatenate([y, v], axis=1)
             return old - product(both, jnp.concatenate([v_others, y_others]))
 
         w_top = shared[:, 3 * part : 4 * part].reshape(width, width)
         w_next = shared[:, 4 * part :].reshape(width, width)
-        w_next = lax.dynamic_slice_in_dim(w_next, own, part, 1)
-        v_top = top + upper
-        x_cols = reduced(c_cols, w_top, v_top, v_cols, y_cols)
-        x_rows = reduced(c_rows, w_top, v_top, v_rows, y_rows)
-        c_own = reduced(later[0], w_next, sums[3 * part :], v_cols, y_cols)
+        v_top = pieces[:, part:].reshape(width, width).T + upper
+        y_top = y_of(w_top, v_top)
+        v_next = sums[3 * part :]
+        y_next = lax.dynamic_slice_in_dim(product(w_next, core, ((0,), (1,))), own, part, 0)
+        y_next = y_next - product(v_next, middle, NT)
+        x_cols = reduced(c_cols, y_top, v_top, v_cols, y_cols)
+        x_rows = reduced(c_rows, y_top, v_top, v_rows, y_rows)
+        c_own = reduced(later[0], y_next, v_next, v_cols, y_cols)
         x_cols = jnp.where(global_cols[None, :] >= start + width, x_cols, 0.0)
         x_rows = jnp.where(global_rows[None, :] >= start + width, x_rows, 0.0)
         c_own = jnp.where(global_cols[None, :] >= start + width, c_own, 0.0)

time: 382 us -> 354 us (0.927)
  the two profiles are of different devices: /device:TPU:2 before, /device:TPU:1 now
where the time goes in v2:
time: 354 us; the launch traced here: 349 us
  waiting for transfers between devices  104 us (29%)
  starting transfers between devices  88.6 us (25%)
  blocking collectives  56.8 us (16%)
  Pallas kernels  38 us (11%)
  local copies, waits for them, and re-layouts  30.4 us (9%)
  matrix products  21.5 us (6%)
  other arithmetic  8.39 us (2%)
    all_to_all x10, waiting for transfers between devices, exchange(): return lax.all_to_all(value, axis, 0, 0, tiled=True)  92.9 us
    all_to_all x10, starting transfers between devices, exchange(): return lax.all_to_all(value, axis, 0, 0, tiled=True)  73.2 us
    all_to_all x2, blocking collectives, exchange(): return lax.all_to_all(value, axis, 0, 0, tiled=True)  56.8 us
    pallas_call x2, Pallas kernels, factor(): pl.pallas_call(functools.partial(factor_kernel, b=32), out_shape=(square,...  38 us
    dot_general x31, matrix products, product(): lax.dot_general(left, right, (dims, ((), ())), precision=precision, prefe...  21.5 us
    ppermute x3, starting transfers between devices, transposed(): return lax.ppermute(row_major(value), ('row', *COL), pairs)  8.88 us
    ppermute x3, waiting for transfers between devices, transposed(): return lax.ppermute(row_major(value), ('row', *COL), pairs)  8.72 us
    broadcast_in_dim x9, local copies, waits for them, and re-layouts, copied(): copies = jnp.broadcast_to(value, (lax.axis_size(axis), *value.shape))  8.19 us
  transfers between devices with their start and end apart: 17, of which 13 were waited for; matrix products, arithmetic and copies ran while one was open for 6% of the time, Pallas kernels for 11%

profile of v2, /device:TPU:1, one launch (start us, length us, event | category | flops | bytes accessed | tf_op | source)
XLA Modules:
  0.0 348.7 jit_solution(7022227229612565461)
XLA Ops:
  0.0 1.2 slice.108
  1.2 1.2 reshape.244
  2.5 7.6 %all-to-all-start = ((f32[16,16,512]{2,1,0:T(8,128)}), f32[16,16,512]{2,1,0:T(8,128)S(1)}, u32[]{:S(2)}, u32[]{:S(2)}) async-start(f32[16,16,512]{2,1,0:T(8,128)} %reshape.244), calls=%async_computation | async-start | bytes 1048576 | tf_op jit(solution)/shard_map/all_to_all | solution.py:151
  10.1 10.4 %all-to-all-done = f32[16,16,512]{2,1,0:T(8,128)S(1)} async-done(((f32[16,16,512]{2,1,0:T(8,128)}), f32[16,16,512]{2,1,0:T(8,128)S(1)}, u32[]{:S(2)}, u32[]{:S(2)}) %all-to-all-start) | async-done | bytes 524320 | tf_op jit(solution)/shard_map/all_to_all | solution.py:151
  20.5 4.1 %collective-permute-start = (f32[16,512]{1,0:T(8,128)S(1)}, f32[16,512]{1,0:T(8,128)S(1)}, u32[]{:S(2)}, u32[]{:S(2)}) collective-permute-start(f32[16,512]{1,0:T(8,128)S(1)} %bitcast_select_fusion), channel_id=1, source_target_pairs={{0,0},{1,16},{2,32},{3,48},{4,64},{5,80},{6,96},{7,112},{8,128},{9... | collective-permute-start | bytes 98312 | tf_op jit(solution)/shard_map/ppermute | solution.py:167
  24.6 1.6 collective-permute-done
  26.9 14.9 %all-to-all-start.1 = ((f32[8,16,512]{2,1,0:T(8,128)}), f32[8,16,512]{2,1,0:T(8,128)S(1)}, u32[]{:S(2)}, u32[]{:S(2)}) async-start(f32[8,16,512]{2,1,0:T(8,128)} %broadcast_in_dim.137), calls=%async_computation.1 | async-start | bytes 524288 | tf_op jit(solution)/shard_map/all_to_all | solution.py:151
  42.0 9.2 %all-to-all-done.1 = f32[8,16,512]{2,1,0:T(8,128)S(1)} async-done(((f32[8,16,512]{2,1,0:T(8,128)}), f32[8,16,512]{2,1,0:T(8,128)S(1)}, u32[]{:S(2)}, u32[]{:S(2)}) %all-to-all-start.1) | async-done | bytes 262176 | tf_op jit(solution)/shard_map/all_to_all | solution.py:151
  51.3 4.1 %collective-permute-start.1 = (f32[8,16,512]{2,1,0:T(8,128)S(1)}, f32[8,16,512]{2,1,0:T(8,128)S(1)}, u32[]{:S(2)}, u32[]{:S(2)}) collective-permute-start(f32[8,16,512]{2,1,0:T(8,128)S(1)} %all-to-all-done.1), channel_id=1, source_target_pairs={{0,1},{1,0},{2,3},{3,2},{4,5},{5,4},{6,7},{7,6},{8,9},{9,8},{10,11... | collective-permute-start | bytes 786440 | tf_op jit(solution)/shard_map/ppermute | solution.py:171
  55.5 1.1 collective-permute-done.1
  58.3 30.4 %all_to_all.60 = f32[16,128,256]{2,1,0:T(8,128)S(1)} all-to-all(f32[16,128,256]{2,1,0:T(8,128)S(1)} %pad_maximum_fusion), channel_id=1, replica_groups=mesh['row'=16,'col_0'=8,'col_1'=2] {'row'}, dimensions={0} | all-to-all | bytes 4194304 | tf_op jit(solution)/shard_map/all_to_all | solution.py:151
  88.7 0.9 slice_reduce_fusion.2
  89.6 0.8 broadcast_in_dim.145
  90.5 5.1 %all-to-all-start.4 = ((f32[16,32,256]{2,1,0:T(8,128)}), f32[16,32,256]{2,1,0:T(8,128)S(1)}, u32[]{:S(2)}, u32[]{:S(2)}) async-start(f32[16,32,256]{2,1,0:T(8,128)} %broadcast_in_dim.145), calls=%async_computation.4 | async-start | bytes 1048576 | tf_op jit(solution)/shard_map/all_to_all | solution.py:151
  95.6 2.3 collective-permute-start.2
  98.0 3.6 %collective-permute-done.2 = f32[2,16,512]{2,1,0:T(8,128)S(1)} collective-permute-done((f32[2,16,512]{2,1,0:T(8,128)S(1)}, f32[2,16,512]{2,1,0:T(8,128)S(1)}, u32[]{:S(2)}, u32[]{:S(2)}) %collective-permute-start.2) | collective-permute-done | bytes 65568 | tf_op jit(solution)/shard_map/ppermute | solution.py:167
  101.5 11.4 %all-to-all-done.4.pieces_ref = f32[16,32,256]{2,1,0:T(8,128)S(1)} async-done(((f32[16,32,256]{2,1,0:T(8,128)}), f32[16,32,256]{2,1,0:T(8,128)S(1)}, u32[]{:S(2)}, u32[]{:S(2)}) %all-to-all-start.4) | async-done | bytes 524320 | tf_op jit(solution)/shard_map/all_to_all | solution.py:151
  112.9 1.0 broadcast_in_dim.144
  113.9 7.0 %all-to-all-start.3 = ((f32[8,2,16,512]{3,2,1,0:T(8,128)}), f32[8,2,16,512]{3,2,1,0:T(8,128)S(1)}, u32[]{:S(2)}, u32[]{:S(2)}) async-start(f32[8,2,16,512]{3,2,1,0:T(8,128)} %broadcast_in_dim.144), calls=%async_computation.3 | async-start | bytes 1048576 | tf_op jit(solution)/shard_map/all_to_all | solution.py:151
  121.7 0.9 copy.105
  122.5 1.2 reshape.251
  124.3 19.1 %factor.2 = (f32[256,256]{1,0:T(8,128)}, f32[256,256]{1,0:T(8,128)}, f32[256,256]{1,0:T(8,128)}) custom-call(f32[16,32,256]{2,1,0:T(8,128)} %copy-done.14), custom_call_target="tpu_custom_call" | custom-call | tf_op jit(solution)/shard_map/factor/pallas_call | solution.py:138
  143.4 1.1 copy.72
  144.5 1.0 convolution_add_fusion.3
  146.5 1.6 collective-permute-start.4
  148.0 0.9 collective-permute-done.4
  149.8 6.9 %all-to-all-start.5 = ((f32[8,64,256]{2,1,0:T(8,128)}), f32[8,64,256]{2,1,0:T(8,128)S(1)}, u32[]{:S(2)}, u32[]{:S(2)}) async-start(f32[8,64,256]{2,1,0:T(8,128)} %broadcast_in_dim.148), calls=%async_computation.5 | async-start | bytes 1048576 | tf_op jit(solution)/shard_map/all_to_all | solution.py:151
  159.1 15.6 %all-to-all-done.5 = f32[8,64,256]{2,1,0:T(8,128)S(1)} async-done(((f32[8,64,256]{2,1,0:T(8,128)}), f32[8,64,256]{2,1,0:T(8,128)S(1)}, u32[]{:S(2)}, u32[]{:S(2)}) %all-to-all-start.5) | async-done | bytes 524320 | tf_op jit(solution)/shard_map/all_to_all | solution.py:151
  174.7 1.2 broadcast_in_dim.149
  176.0 5.3 %all-to-all-start.6 = ((f32[16,80,256]{2,1,0:T(8,128)}), f32[16,80,256]{2,1,0:T(8,128)S(1)}, u32[]{:S(2)}, u32[]{:S(2)}) async-start(f32[16,80,256]{2,1,0:T(8,128)} %broadcast_in_dim.149), calls=%async_computation.6 | async-start | bytes 2621440 | tf_op jit(solution)/shard_map/all_to_all | solution.py:151
  181.2 1.8 bitcast_add_fusion
  183.0 1.2 select_bitcast_fusion.3
  185.7 1.4 fusion.86
  187.1 13.9 %all-to-all-done.6 = f32[16,80,256]{2,1,0:T(8,128)S(1)} async-done(((f32[16,80,256]{2,1,0:T(8,128)}), f32[16,80,256]{2,1,0:T(8,128)S(1)}, u32[]{:S(2)}, u32[]{:S(2)}) %all-to-all-start.6) | async-done | bytes 1310752 | tf_op jit(solution)/shard_map/all_to_all | solution.py:151
  201.7 1.1 fusion.84
  204.3 1.2 reshape.258
  207.2 1.3 fusion.6
  209.1 2.2 convolution_subtract_fusion.1
  212.9 1.4 fusion.89
  214.3 1.1 reshape.260
  215.7 26.3 %all_to_all.61 = f32[16,96,256]{2,1,0:T(8,128)S(1)} all-to-all(f32[16,96,256]{2,1,0:T(8,128)S(1)} %pad_maximum_fusion.1), channel_id=1, replica_groups=mesh['row'=16,'col_0'=8,'col_1'=2] {'row'}, dimensions={0} | all-to-all | bytes 3145728 | tf_op jit(solution)/shard_map/all_to_all | solution.py:151
  242.1 0.9 slice_reduce_fusion
  243.0 0.8 broadcast_in_dim.154
  243.8 5.4 %all-to-all-start.9 = ((f32[16,32,256]{2,1,0:T(8,128)}), f32[16,32,256]{2,1,0:T(8,128)S(1)}, u32[]{:S(2)}, u32[]{:S(2)}) async-start(f32[16,32,256]{2,1,0:T(8,128)} %broadcast_in_dim.154), calls=%async_computation.9 | async-start | bytes 1048576 | tf_op jit(solution)/shard_map/all_to_all | solution.py:151
  249.2 2.4 collective-permute-start.5
  251.7 3.6 %collective-permute-done.5 = f32[2,16,512]{2,1,0:T(8,128)S(1)} collective-permute-done((f32[2,16,512]{2,1,0:T(8,128)S(1)}, f32[2,16,512]{2,1,0:T(8,128)S(1)}, u32[]{:S(2)}, u32[]{:S(2)}) %collective-permute-start.5) | collective-permute-done | bytes 65568 | tf_op jit(solution)/shard_map/ppermute | solution.py:167
  255.2 11.2 %all-to-all-done.9.pieces_ref = f32[16,32,256]{2,1,0:T(8,128)S(1)} async-done(((f32[16,32,256]{2,1,0:T(8,128)}), f32[16,32,256]{2,1,0:T(8,128)S(1)}, u32[]{:S(2)}, u32[]{:S(2)}) %all-to-all-start.9) | async-done | bytes 524320 | tf_op jit(solution)/shard_map/all_to_all | solution.py:151
  266.5 1.0 broadcast_in_dim.153
  267.5 7.0 %all-to-all-start.8 = ((f32[8,2,16,512]{3,2,1,0:T(8,128)}), f32[8,2,16,512]{3,2,1,0:T(8,128)S(1)}, u32[]{:S(2)}, u32[]{:S(2)}) async-start(f32[8,2,16,512]{3,2,1,0:T(8,128)} %broadcast_in_dim.153), calls=%async_computation.8 | async-start | bytes 1048576 | tf_op jit(solution)/shard_map/all_to_all | solution.py:151
  274.5 1.0 copy.88
  275.5 1.7 fusion.5
  277.2 1.2 reshape.264
  278.4 18.9 %factor.3 = (f32[256,256]{1,0:T(8,128)}, f32[256,256]{1,0:T(8,128)}, f32[256,256]{1,0:T(8,128)}) custom-call(f32[16,32,256]{2,1,0:T(8,128)} %copy-done.20), custom_call_target="tpu_custom_call" | custom-call | tf_op jit(solution)/shard_map/factor/pallas_call | solution.py:138
  297.3 1.1 copy.90
  299.8 8.7 %all-to-all-start.10 = ((f32[16,16,256]{2,1,0:T(8,128)}), f32[16,16,256]{2,1,0:T(8,128)S(1)}, u32[]{:S(2)}, u32[]{:S(2)}) async-start(f32[16,16,256]{2,1,0:T(8,128)} %broadcast_in_dim.157), calls=%async_computation.10 | async-start | bytes 524288 | tf_op jit(solution)/shard_map/all_to_all | solution.py:151
  308.7 0.9 copy.86
  310.4 0.8 slice_add_fusion
  311.3 8.8 %all-to-all-done.10 = f32[16,16,256]{2,1,0:T(8,128)S(1)} async-done(((f32[16,16,256]{2,1,0:T(8,128)}), f32[16,16,256]{2,1,0:T(8,128)S(1)}, u32[]{:S(2)}, u32[]{:S(2)}) %all-to-all-start.10) | async-done | bytes 262176 | tf_op jit(solution)/shard_map/all_to_all | solution.py:151
  320.1 1.0 broadcast_in_dim.158
  321.1 5.3 %all-to-all-start.11 = ((f32[16,48,256]{2,1,0:T(8,128)}), f32[16,48,256]{2,1,0:T(8,128)S(1)}, u32[]{:S(2)}, u32[]{:S(2)}) async-start(f32[16,48,256]{2,1,0:T(8,128)} %broadcast_in_dim.158), calls=%async_computation.11 | async-start | bytes 1572864 | tf_op jit(solution)/shard_map/all_to_all | solution.py:151
  326.4 1.1 select_bitcast_fusion.1
  329.1 12.3 %all-to-all-done.11 = f32[16,48,256]{2,1,0:T(8,128)S(1)} async-done(((f32[16,48,256]{2,1,0:T(8,128)}), f32[16,48,256]{2,1,0:T(8,128)S(1)}, u32[]{:S(2)}, u32[]{:S(2)}) %all-to-all-start.11) | async-done | bytes 786464 | tf_op jit(solution)/shard_map/all_to_all | solution.py:151
  344.4 2.4 fusion.3
  346.8 1.6 reshape.268
  (171 shorter events, 22.4 us)
Async XLA Ops:
  1.2 40.7 %copy-start.16 = (f32[2,256,2,256]{3,2,1,0:T(2,128)S(1)}, f32[2,256,2,256]{3,2,1,0:T(2,128)}, u32[]{:S(2)}) copy-start(f32[2,256,2,256]{3,2,1,0:T(2,128)} %param.1) | copy-start | bytes 3145732
  2.5 18.0 %all-to-all-start = ((f32[16,16,512]{2,1,0:T(8,128)}), f32[16,16,512]{2,1,0:T(8,128)S(1)}, u32[]{:S(2)}, u32[]{:S(2)}) async-start(f32[16,16,512]{2,1,0:T(8,128)} %reshape.244), calls=%async_computation | async-start | bytes 1048576 | tf_op jit(solution)/shard_map/all_to_all | solution.py:151
  20.5 34.9 %copy-start.30 = (f32[16,16,512]{2,1,0:T(8,128)}, f32[16,16,512]{2,1,0:T(8,128)S(1)}, u32[]{:S(2)}) copy-start(f32[16,16,512]{2,1,0:T(8,128)S(1)} %all-to-all-done) | copy-start | bytes 1572868
  20.5 5.7 %collective-permute-start = (f32[16,512]{1,0:T(8,128)S(1)}, f32[16,512]{1,0:T(8,128)S(1)}, u32[]{:S(2)}, u32[]{:S(2)}) collective-permute-start(f32[16,512]{1,0:T(8,128)S(1)} %bitcast_select_fusion), channel_id=1, source_target_pairs={{0,0},{1,16},{2,32},{3,48},{4,64},{5,80},{6,96},{7,112},{8,128},{9... | collective-permute-start | bytes 98312 | tf_op jit(solution)/shard_map/ppermute | solution.py:167
  26.9 24.3 %all-to-all-start.1 = ((f32[8,16,512]{2,1,0:T(8,128)}), f32[8,16,512]{2,1,0:T(8,128)S(1)}, u32[]{:S(2)}, u32[]{:S(2)}) async-start(f32[8,16,512]{2,1,0:T(8,128)} %broadcast_in_dim.137), calls=%async_computation.1 | async-start | bytes 524288 | tf_op jit(solution)/shard_map/all_to_all | solution.py:151
  51.3 5.3 %collective-permute-start.1 = (f32[8,16,512]{2,1,0:T(8,128)S(1)}, f32[8,16,512]{2,1,0:T(8,128)S(1)}, u32[]{:S(2)}, u32[]{:S(2)}) collective-permute-start(f32[8,16,512]{2,1,0:T(8,128)S(1)} %all-to-all-done.1), channel_id=1, source_target_pairs={{0,1},{1,0},{2,3},{3,2},{4,5},{5,4},{6,7},{7,6},{8,9},{9,8},{10,11... | collective-permute-start | bytes 786440 | tf_op jit(solution)/shard_map/ppermute | solution.py:171
  90.5 22.4 %all-to-all-start.4 = ((f32[16,32,256]{2,1,0:T(8,128)}), f32[16,32,256]{2,1,0:T(8,128)S(1)}, u32[]{:S(2)}, u32[]{:S(2)}) async-start(f32[16,32,256]{2,1,0:T(8,128)} %broadcast_in_dim.145), calls=%async_computation.4 | async-start | bytes 1048576 | tf_op jit(solution)/shard_map/all_to_all | solution.py:151
  95.6 5.9 %collective-permute-start.2 = (f32[2,16,512]{2,1,0:T(8,128)S(1)}, f32[2,16,512]{2,1,0:T(8,128)S(1)}, u32[]{:S(2)}, u32[]{:S(2)}) collective-permute-start(f32[2,16,512]{2,1,0:T(8,128)S(1)} %pad_maximum_fusion.20), channel_id=1, source_target_pairs={{0,0},{1,16},{2,32},{3,48},{4,64},{5,80},{6,96},{7,112},{8,128},{9... | collective-permute-start | bytes 196616 | tf_op jit(solution)/shard_map/ppermute | solution.py:167
  112.9 9.6 %copy-start.14 = (f32[16,32,256]{2,1,0:T(8,128)}, f32[16,32,256]{2,1,0:T(8,128)S(1)}, u32[]{:S(2)}) copy-start(f32[16,32,256]{2,1,0:T(8,128)S(1)} %all-to-all-done.4.pieces_ref) | copy-start | bytes 1572868
  113.9 29.5 %all-to-all-start.3 = ((f32[8,2,16,512]{3,2,1,0:T(8,128)}), f32[8,2,16,512]{3,2,1,0:T(8,128)S(1)}, u32[]{:S(2)}, u32[]{:S(2)}) async-start(f32[8,2,16,512]{3,2,1,0:T(8,128)} %broadcast_in_dim.144), calls=%async_computation.3 | async-start | bytes 1048576 | tf_op jit(solution)/shard_map/all_to_all | solution.py:151
  123.7 20.7 %copy-start.1 = (f32[256,512]{1,0:T(8,128)}, f32[256,512]{1,0:T(8,128)S(1)}, u32[]{:S(2)}) copy-start(f32[256,512]{1,0:T(8,128)S(1)} %reshape.251) | copy-start | bytes 1572868
  124.0 21.5 %copy-start.29 = (f32[256,256]{0,1:T(8,128)S(1)}, f32[256,256]{0,1:T(8,128)}, u32[]{:S(2)}) copy-start(f32[256,256]{0,1:T(8,128)} %copy.105) | copy-start | bytes 786436
  146.2 11.2 %copy-start.28 = (f32[256,256]{1,0:T(8,128)S(1)}, f32[256,256]{1,0:T(8,128)}, u32[]{:S(2)}) copy-start(f32[256,256]{1,0:T(8,128)} %get-tuple-element.61) | copy-start | bytes 786436
  146.4 11.9 %slice-start = ((f32[16,32,256]{2,1,0:T(8,128)}), f32[16,16,256]{2,1,0:T(8,128)S(1)}, s32[]{:S(2)}) async-start(f32[16,32,256]{2,1,0:T(8,128)} %copy-done.14), calls=%async_computation.12 | async-start | bytes 524288 | tf_op jit(solution)/shard_map/slice | solution.py:287
  146.5 2.5 collective-permute-start.4
  149.8 24.9 %all-to-all-start.5 = ((f32[8,64,256]{2,1,0:T(8,128)}), f32[8,64,256]{2,1,0:T(8,128)S(1)}, u32[]{:S(2)}, u32[]{:S(2)}) async-start(f32[8,64,256]{2,1,0:T(8,128)} %broadcast_in_dim.148), calls=%async_computation.5 | async-start | bytes 1048576 | tf_op jit(solution)/shard_map/all_to_all | solution.py:151
  156.7 26.3 %collective-permute-start.3 = (f32[8,2,16,512]{3,2,1,0:T(8,128)S(1)}, f32[8,2,16,512]{3,2,1,0:T(8,128)}, u32[]{:S(2)}, u32[]{:S(2)}) collective-permute-start(f32[8,2,16,512]{3,2,1,0:T(8,128)S(1)} %all-to-all-done.3), channel_id=1, source_target_pairs={{0,1},{1,0},{2,3},{3,2},{4,5},{5,4},{6,7},{7,6},{8,9},{9,8},{10,11... | collective-permute-start | bytes 1572872 | tf_op jit(solution)/shard_map/ppermute | solution.py:171
  176.0 25.0 %all-to-all-start.6 = ((f32[16,80,256]{2,1,0:T(8,128)}), f32[16,80,256]{2,1,0:T(8,128)S(1)}, u32[]{:S(2)}, u32[]{:S(2)}) async-start(f32[16,80,256]{2,1,0:T(8,128)} %broadcast_in_dim.149), calls=%async_computation.6 | async-start | bytes 2621440 | tf_op jit(solution)/shard_map/all_to_all | solution.py:151
  184.3 1.0 copy-start.21
  184.3 1.4 copy-start
  184.4 2.7 copy-start.3
  204.3 1.9 copy-start.27
  206.6 2.0 copy-start.6
  206.6 2.0 copy-start.10
  206.6 2.0 copy-start.19
  209.0 2.2 copy-start.12
  209.1 2.2 copy-start.26
  209.1 2.6 copy-start.4
  209.1 2.6 copy-start.7
  209.1 2.6 copy-start.11
  211.3 1.6 copy-start.8
  211.6 1.2 copy-start.17
  243.8 30.7 %copy-start.2 = (f32[256,512]{1,0:T(8,128)S(1)}, f32[256,512]{1,0:T(8,128)}, u32[]{:S(2)}) copy-start(f32[256,512]{1,0:T(8,128)} %copy-done.1) | copy-start | bytes 1572868
  243.8 22.7 %all-to-all-start.9 = ((f32[16,32,256]{2,1,0:T(8,128)}), f32[16,32,256]{2,1,0:T(8,128)S(1)}, u32[]{:S(2)}, u32[]{:S(2)}) async-start(f32[16,32,256]{2,1,0:T(8,128)} %broadcast_in_dim.154), calls=%async_computation.9 | async-start | bytes 1048576 | tf_op jit(solution)/shard_map/all_to_all | solution.py:151
  249.2 26.4 %copy-start.13 = (f32[256,256]{1,0:T(8,128)S(1)}, f32[256,256]{1,0:T(8,128)}, u32[]{:S(2)}) copy-start(f32[256,256]{1,0:T(8,128)} %bitcast_add_fusion) | copy-start | bytes 786436
  249.2 26.3 %copy-start.18 = (f32[256,256]{1,0:T(8,128)S(1)}, f32[256,256]{1,0:T(8,128)}, u32[]{:S(2)}) copy-start(f32[256,256]{1,0:T(8,128)} %copy-done.17) | copy-start | bytes 786436
  249.2 6.0 %collective-permute-start.5 = (f32[2,16,512]{2,1,0:T(8,128)S(1)}, f32[2,16,512]{2,1,0:T(8,128)S(1)}, u32[]{:S(2)}, u32[]{:S(2)}) collective-permute-start(f32[2,16,512]{2,1,0:T(8,128)S(1)} %pad_maximum_fusion.23), channel_id=1, source_target_pairs={{0,0},{1,16},{2,32},{3,48},{4,64},{5,80},{6,96},{7,112},{8,128},{9... | collective-permute-start | bytes 196616 | tf_op jit(solution)/shard_map/ppermute | solution.py:167
  266.5 1.0 copy-start.20
  267.5 29.8 %all-to-all-start.8 = ((f32[8,2,16,512]{3,2,1,0:T(8,128)}), f32[8,2,16,512]{3,2,1,0:T(8,128)S(1)}, u32[]{:S(2)}, u32[]{:S(2)}) async-start(f32[8,2,16,512]{3,2,1,0:T(8,128)} %broadcast_in_dim.153), calls=%async_computation.8 | async-start | bytes 1048576 | tf_op jit(solution)/shard_map/all_to_all | solution.py:151
  297.3 1.2 copy-start.15
  298.5 10.2 %copy-start.24 = (f32[256,256]{1,0:T(8,128)S(1)}, f32[256,256]{1,0:T(8,128)}, u32[]{:S(2)}) copy-start(f32[256,256]{1,0:T(8,128)} %get-tuple-element.25) | copy-start | bytes 786436
  298.6 11.0 %copy-start.31 = (f32[256,256]{1,0:T(8,128)S(1)}, f32[256,256]{1,0:T(8,128)}, u32[]{:S(2)}) copy-start(f32[256,256]{1,0:T(8,128)} %get-tuple-element.29) | copy-start | bytes 786436
  299.8 20.3 %all-to-all-start.10 = ((f32[16,16,256]{2,1,0:T(8,128)}), f32[16,16,256]{2,1,0:T(8,128)S(1)}, u32[]{:S(2)}, u32[]{:S(2)}) async-start(f32[16,16,256]{2,1,0:T(8,128)} %broadcast_in_dim.157), calls=%async_computation.10 | async-start | bytes 524288 | tf_op jit(solution)/shard_map/all_to_all | solution.py:151
  308.5 17.9 %collective-permute-start.6 = (f32[8,2,16,512]{3,2,1,0:T(8,128)S(1)}, f32[8,2,16,512]{3,2,1,0:T(8,128)}, u32[]{:S(2)}, u32[]{:S(2)}) collective-permute-start(f32[8,2,16,512]{3,2,1,0:T(8,128)S(1)} %all-to-all-done.8), channel_id=1, source_target_pairs={{0,1},{1,0},{2,3},{3,2},{4,5},{5,4},{6,7},{7,6},{8,9},{9,8},{10,11... | collective-permute-start | bytes 1572872 | tf_op jit(solution)/shard_map/ppermute | solution.py:171
  321.1 20.3 %all-to-all-start.11 = ((f32[16,48,256]{2,1,0:T(8,128)}), f32[16,48,256]{2,1,0:T(8,128)S(1)}, u32[]{:S(2)}, u32[]{:S(2)}) async-start(f32[16,48,256]{2,1,0:T(8,128)} %broadcast_in_dim.158), calls=%async_computation.11 | async-start | bytes 1572864 | tf_op jit(solution)/shard_map/all_to_all | solution.py:151
  327.8 1.0 copy-start.5
  342.2 1.1 copy-start.22
  342.2 1.1 copy-start.23
  342.9 1.3 copy-start.9
  342.9 1.3 copy-start.25
  342.9 1.4 copy-start.32
  342.9 1.4 copy-start.33
  342.9 1.5 copy-start.34

commit v3 on v2

--- a/solution.py
+++ b/solution.py
@@ -235,11 +235,14 @@
             x_cols = merged[:, 4 * part : 6 * part].reshape(width, local)
         u_own = jnp.sum(merged[:, -2 * part :], axis=0).reshape(part, local)
         u_own = jnp.where(below_cols, u_own, 0.0)
-        pair = transposed(jnp.stack([u_own, c_own]))
-        pair = copied(pair, COL[0])
-        factors = factor(pieces)
-        pair, (upper, lower, core) = lax.optimization_barrier((pair, factors))
-        u_rows, c_rows = join(both_cores(pair))
+        if last:
+            upper, lower, core = factor(pieces)
+        else:
+            pair = transposed(jnp.stack([u_own, c_own]))
+            pair = copied(pair, COL[0])
+            factors = factor(pieces)
+            pair, (upper, lower, core) = lax.optimization_barrier((pair, factors))
+            u_rows, c_rows = join(both_cores(pair))
 
         def with_top(x, index):
             head = jnp.where(index == panel + 1, lower, 0.0)
@@ -248,19 +251,23 @@
         v_cols = with_top(x_cols, col_index)
         v_rows = with_top(x_rows, row_index)
         w_own = u_own + product(lax.dynamic_slice_in_dim(lower, own, part, 0), c_cols)
-        w_rows = u_rows + product(lower, c_rows)
         parts = [product(w_own, v_cols, NT)]
-        if not last:
+        if last:
+            turned = transposed(w_own)
+            own_sum = core_sum(row_major(parts[0])).reshape(part // 2, local)
+            lines = copied(jnp.concatenate([turned, own_sum]), COL[0])
+            sums = jnp.sum(lines[:, part:], axis=0).reshape(part, width)
+            w_rows = both_cores(lines[:, :part]).reshape(width, local)
+        else:
+            w_rows = u_rows + product(lower, c_rows)
             across = lax.dynamic_slice_in_dim(x_cols[:, :width].T, own, part, 0)
             parts += [
                 jnp.where(col_index == panel + 1, w_own[:, :width], 0.0),
                 jnp.where(col_index == panel + 2, w_own[:, :width], 0.0),
                 jnp.where(col_index == panel + 2, across, 0.0),
             ]
-        if last:
-            sums = jnp.sum(copied(parts[0], COL), axis=0)
-        else:
-            sums = jnp.sum(copied(core_sum(row_major(jnp.concatenate(parts))), COL[0]), axis=0)
+            sums = core_sum(row_major(jnp.concatenate(parts)))
+            sums = jnp.sum(copied(sums, COL[0]), axis=0)
         shared = jnp.concatenate([w_own.reshape(2 * part, width), sums[: 3 * part]])
         shared = copied(shared, "row")
         w_cols = shared[:, : 2 * part].reshape(width, local)

time: 354 us -> 352 us (level)
  the two profiles are of different devices: /device:TPU:1 before, /device:TPU:2 now
where the time goes in v3:
time: 352 us; the launch traced here: 346 us
  waiting for transfers between devices  101 us (29%)
  starting transfers between devices  79.2 us (22%)
  blocking collectives  59.4 us (17%)
  Pallas kernels  38 us (11%)
  local copies, waits for them, and re-layouts  32.4 us (9%)
  matrix products  25.5 us (7%)
  other arithmetic  9.1 us (3%)
    all_to_all x9, waiting for transfers between devices, exchange(): return lax.all_to_all(value, axis, 0, 0, tiled=True)  91.2 us
    all_to_all x9, starting transfers between devices, exchange(): return lax.all_to_all(value, axis, 0, 0, tiled=True)  69.1 us
    all_to_all x2, blocking collectives, exchange(): return lax.all_to_all(value, axis, 0, 0, tiled=True)  59.4 us
    pallas_call x2, Pallas kernels, factor(): pl.pallas_call(functools.partial(factor_kernel, b=32), out_shape=(square,...  38 us
    dot_general x30, matrix products, product(): lax.dot_general(left, right, (dims, ((), ())), precision=precision, prefe...  25.5 us
    ppermute x3, starting transfers between devices, transposed(): return lax.ppermute(row_major(value), ('row', *COL), pairs)  9.85 us
    broadcast_in_dim x8, local copies, waits for them, and re-layouts, copied(): copies = jnp.broadcast_to(value, (lax.axis_size(axis), *value.shape))  7.26 us
  transfers between devices with their start and end apart: 17, of which 13 were waited for; matrix products, arithmetic and copies ran while one was open for 8% of the time, Pallas kernels for 6%

profile of v3, /device:TPU:2, one launch (start us, length us, event | category | flops | bytes accessed | tf_op | source)
XLA Modules:
  0.0 345.7 jit_solution(4638451439714096499)
XLA Ops:
  0.0 1.2 slice.108
  1.2 1.2 reshape.217
  2.5 7.5 %all-to-all-start = ((f32[16,16,512]{2,1,0:T(8,128)}), f32[16,16,512]{2,1,0:T(8,128)S(1)}, u32[]{:S(2)}, u32[]{:S(2)}) async-start(f32[16,16,512]{2,1,0:T(8,128)} %reshape.217), calls=%async_computation | async-start | bytes 1048576 | tf_op jit(solution)/shard_map/all_to_all | solution.py:151
  9.9 10.2 %all-to-all-done = f32[16,16,512]{2,1,0:T(8,128)S(1)} async-done(((f32[16,16,512]{2,1,0:T(8,128)}), f32[16,16,512]{2,1,0:T(8,128)S(1)}, u32[]{:S(2)}, u32[]{:S(2)}) %all-to-all-start) | async-done | bytes 524320 | tf_op jit(solution)/shard_map/all_to_all | solution.py:151
  20.1 1.9 collective-permute-start
  22.0 3.3 collective-permute-done
  26.1 15.8 %all-to-all-start.1 = ((f32[8,16,512]{2,1,0:T(8,128)}), f32[8,16,512]{2,1,0:T(8,128)S(1)}, u32[]{:S(2)}, u32[]{:S(2)}) async-start(f32[8,16,512]{2,1,0:T(8,128)} %broadcast_in_dim.131), calls=%async_computation.1 | async-start | bytes 524288 | tf_op jit(solution)/shard_map/all_to_all | solution.py:151
  42.0 10.3 %all-to-all-done.1 = f32[8,16,512]{2,1,0:T(8,128)S(1)} async-done(((f32[8,16,512]{2,1,0:T(8,128)}), f32[8,16,512]{2,1,0:T(8,128)S(1)}, u32[]{:S(2)}, u32[]{:S(2)}) %all-to-all-start.1) | async-done | bytes 262176 | tf_op jit(solution)/shard_map/all_to_all | solution.py:151
  52.4 1.5 collective-permute-done.1
  55.8 32.5 %all_to_all.55 = f32[16,128,256]{2,1,0:T(8,128)S(1)} all-to-all(f32[16,128,256]{2,1,0:T(8,128)S(1)} %pad_maximum_fusion), channel_id=1, replica_groups=mesh['row'=16,'col_0'=8,'col_1'=2] {'row'}, dimensions={0} | all-to-all | bytes 4194304 | tf_op jit(solution)/shard_map/all_to_all | solution.py:151
  88.2 0.9 slice_reduce_fusion.2
  89.2 0.9 broadcast_in_dim.139
  90.0 3.6 %all-to-all-start.4 = ((f32[16,32,256]{2,1,0:T(8,128)}), f32[16,32,256]{2,1,0:T(8,128)S(1)}, u32[]{:S(2)}, u32[]{:S(2)}) async-start(f32[16,32,256]{2,1,0:T(8,128)} %broadcast_in_dim.139), calls=%async_computation.4 | async-start | bytes 1048576 | tf_op jit(solution)/shard_map/all_to_all | solution.py:151
  93.7 3.3 collective-permute-start.2
  96.9 2.3 collective-permute-done.2
  99.2 11.0 %all-to-all-done.4.pieces_ref = f32[16,32,256]{2,1,0:T(8,128)S(1)} async-done(((f32[16,32,256]{2,1,0:T(8,128)}), f32[16,32,256]{2,1,0:T(8,128)S(1)}, u32[]{:S(2)}, u32[]{:S(2)}) %all-to-all-start.4) | async-done | bytes 524320 | tf_op jit(solution)/shard_map/all_to_all | solution.py:151
  110.2 1.0 broadcast_in_dim.138
  111.2 5.5 %all-to-all-start.3 = ((f32[8,2,16,512]{3,2,1,0:T(8,128)}), f32[8,2,16,512]{3,2,1,0:T(8,128)S(1)}, u32[]{:S(2)}, u32[]{:S(2)}) async-start(f32[8,2,16,512]{3,2,1,0:T(8,128)} %broadcast_in_dim.138), calls=%async_computation.3 | async-start | bytes 1048576 | tf_op jit(solution)/shard_map/all_to_all | solution.py:151
  118.4 1.2 reshape.224
  120.1 19.1 %factor.2 = (f32[256,256]{1,0:T(8,128)}, f32[256,256]{1,0:T(8,128)}, f32[256,256]{1,0:T(8,128)}) custom-call(f32[16,32,256]{2,1,0:T(8,128)} %copy-done.8), custom_call_target="tpu_custom_call" | custom-call | tf_op jit(solution)/shard_map/factor/pallas_call | solution.py:138
  139.2 1.1 copy.96
  140.3 1.0 convolution_add_fusion.2
  142.5 1.2 collective-permute-done.4
  144.6 7.2 %all-to-all-start.5 = ((f32[8,64,256]{2,1,0:T(8,128)}), f32[8,64,256]{2,1,0:T(8,128)S(1)}, u32[]{:S(2)}, u32[]{:S(2)}) async-start(f32[8,64,256]{2,1,0:T(8,128)} %broadcast_in_dim.142), calls=%async_computation.5 | async-start | bytes 1048576 | tf_op jit(solution)/shard_map/all_to_all | solution.py:151
  151.9 0.9 copy.141
  153.6 16.0 %all-to-all-done.5 = f32[8,64,256]{2,1,0:T(8,128)S(1)} async-done(((f32[8,64,256]{2,1,0:T(8,128)}), f32[8,64,256]{2,1,0:T(8,128)S(1)}, u32[]{:S(2)}, u32[]{:S(2)}) %all-to-all-start.5) | async-done | bytes 524320 | tf_op jit(solution)/shard_map/all_to_all | solution.py:151
  169.7 1.2 broadcast_in_dim.143
  170.9 10.4 %all-to-all-start.6 = ((f32[16,80,256]{2,1,0:T(8,128)}), f32[16,80,256]{2,1,0:T(8,128)S(1)}, u32[]{:S(2)}, u32[]{:S(2)}) async-start(f32[16,80,256]{2,1,0:T(8,128)} %broadcast_in_dim.143), calls=%async_computation.6 | async-start | bytes 2621440 | tf_op jit(solution)/shard_map/all_to_all | solution.py:151
  181.3 1.8 bitcast_add_fusion
  183.1 1.2 select_bitcast_fusion.1
  184.5 1.1 fusion.78
  185.6 2.1 copy.109
  187.7 1.6 convolution_add_fusion
  189.3 1.4 fusion.86
  190.7 9.5 %all-to-all-done.6 = f32[16,80,256]{2,1,0:T(8,128)S(1)} async-done(((f32[16,80,256]{2,1,0:T(8,128)}), f32[16,80,256]{2,1,0:T(8,128)S(1)}, u32[]{:S(2)}, u32[]{:S(2)}) %all-to-all-start.6) | async-done | bytes 1310752 | tf_op jit(solution)/shard_map/all_to_all | solution.py:151
  201.0 1.1 fusion.87
  202.7 0.9 slice.163
  203.5 1.2 reshape.231
  205.4 0.9 convolution_subtract_fusion.10
  207.1 1.3 fusion.6
  208.8 1.5 convolution_subtract_fusion.7
  210.4 2.0 convolution_subtract_fusion.1
  214.3 1.9 fusion.89
  216.5 27.0 %all_to_all.56 = f32[16,96,256]{2,1,0:T(8,128)S(1)} all-to-all(f32[16,96,256]{2,1,0:T(8,128)S(1)} %pad_maximum_fusion.1), channel_id=1, replica_groups=mesh['row'=16,'col_0'=8,'col_1'=2] {'row'}, dimensions={0} | all-to-all | bytes 3145728 | tf_op jit(solution)/shard_map/all_to_all | solution.py:151
  243.4 0.9 slice_reduce_fusion
  244.4 0.9 broadcast_in_dim.147
  245.2 3.7 %all-to-all-start.8 = ((f32[16,32,256]{2,1,0:T(8,128)}), f32[16,32,256]{2,1,0:T(8,128)S(1)}, u32[]{:S(2)}, u32[]{:S(2)}) async-start(f32[16,32,256]{2,1,0:T(8,128)} %broadcast_in_dim.147), calls=%async_computation.8 | async-start | bytes 1048576 | tf_op jit(solution)/shard_map/all_to_all | solution.py:151
  249.0 1.0 copy.116
  250.0 2.5 fusion.5
  252.4 1.3 reshape.235
  253.7 11.0 %all-to-all-done.8.pieces_ref = f32[16,32,256]{2,1,0:T(8,128)S(1)} async-done(((f32[16,32,256]{2,1,0:T(8,128)}), f32[16,32,256]{2,1,0:T(8,128)S(1)}, u32[]{:S(2)}, u32[]{:S(2)}) %all-to-all-start.8) | async-done | bytes 524320 | tf_op jit(solution)/shard_map/all_to_all | solution.py:151
  265.5 18.9 %factor.3 = (f32[256,256]{1,0:T(8,128)}, f32[256,256]{1,0:T(8,128)}, f32[256,256]{1,0:T(8,128)}) custom-call(f32[16,32,256]{2,1,0:T(8,128)} %copy-done.12), custom_call_target="tpu_custom_call" | custom-call | tf_op jit(solution)/shard_map/factor/pallas_call | solution.py:138
  284.4 1.1 copy.118
  285.5 1.0 convolution_add_fusion.1
  286.4 4.7 %collective-permute-start.5 = (f32[16,512]{1,0:T(8,128)S(1)}, f32[16,512]{1,0:T(8,128)S(1)}, u32[]{:S(2)}, u32[]{:S(2)}) collective-permute-start(f32[16,512]{1,0:T(8,128)S(1)} %convolution_add_fusion.1), channel_id=1, source_target_pairs={{0,0},{1,16},{2,32},{3,48},{4,64},{5,80},{6,96},{7,112},{8,128},{9... | collective-permute-start | bytes 98312 | tf_op jit(solution)/shard_map/ppermute | solution.py:167
  291.1 0.9 slice_add_fusion.1
  292.3 1.2 collective-permute-done.6
  294.3 9.5 %all-to-all-start.9 = ((f32[8,24,512]{2,1,0:T(8,128)}), f32[8,24,512]{2,1,0:T(8,128)S(1)}, u32[]{:S(2)}, u32[]{:S(2)}) async-start(f32[8,24,512]{2,1,0:T(8,128)} %broadcast_in_dim.150), calls=%async_computation.9 | async-start | bytes 786432 | tf_op jit(solution)/shard_map/all_to_all | solution.py:151
  305.0 13.5 %all-to-all-done.9 = f32[8,24,512]{2,1,0:T(8,128)S(1)} async-done(((f32[8,24,512]{2,1,0:T(8,128)}), f32[8,24,512]{2,1,0:T(8,128)S(1)}, u32[]{:S(2)}, u32[]{:S(2)}) %all-to-all-start.9) | async-done | bytes 393248 | tf_op jit(solution)/shard_map/all_to_all | solution.py:151
  318.7 1.0 broadcast_in_dim.151
  319.7 5.8 %all-to-all-start.10 = ((f32[16,48,256]{2,1,0:T(8,128)}), f32[16,48,256]{2,1,0:T(8,128)S(1)}, u32[]{:S(2)}, u32[]{:S(2)}) async-start(f32[16,48,256]{2,1,0:T(8,128)} %broadcast_in_dim.151), calls=%async_computation.10 | async-start | bytes 1572864 | tf_op jit(solution)/shard_map/all_to_all | solution.py:151
  329.4 9.8 %all-to-all-done.10 = f32[16,48,256]{2,1,0:T(8,128)S(1)} async-done(((f32[16,48,256]{2,1,0:T(8,128)}), f32[16,48,256]{2,1,0:T(8,128)S(1)}, u32[]{:S(2)}, u32[]{:S(2)}) %all-to-all-start.10) | async-done | bytes 786464 | tf_op jit(solution)/shard_map/all_to_all | solution.py:151
  342.2 1.6 fusion.3
  343.8 1.6 reshape.242
  (178 shorter events, 23.3 us)
Async XLA Ops:
  1.2 40.7 %copy-start.9 = (f32[2,256,2,256]{3,2,1,0:T(2,128)S(1)}, f32[2,256,2,256]{3,2,1,0:T(2,128)}, u32[]{:S(2)}) copy-start(f32[2,256,2,256]{3,2,1,0:T(2,128)} %param.1) | copy-start | bytes 3145732
  2.5 17.6 %all-to-all-start = ((f32[16,16,512]{2,1,0:T(8,128)}), f32[16,16,512]{2,1,0:T(8,128)S(1)}, u32[]{:S(2)}, u32[]{:S(2)}) async-start(f32[16,16,512]{2,1,0:T(8,128)} %reshape.217), calls=%async_computation | async-start | bytes 1048576 | tf_op jit(solution)/shard_map/all_to_all | solution.py:151
  20.1 32.3 %copy-start.23 = (f32[16,16,512]{2,1,0:T(8,128)}, f32[16,16,512]{2,1,0:T(8,128)S(1)}, u32[]{:S(2)}) copy-start(f32[16,16,512]{2,1,0:T(8,128)S(1)} %all-to-all-done) | copy-start | bytes 1572868
  20.1 5.2 %collective-permute-start = (f32[16,512]{1,0:T(8,128)S(1)}, f32[16,512]{1,0:T(8,128)S(1)}, u32[]{:S(2)}, u32[]{:S(2)}) collective-permute-start(f32[16,512]{1,0:T(8,128)S(1)} %bitcast_select_fusion), channel_id=1, source_target_pairs={{0,0},{1,16},{2,32},{3,48},{4,64},{5,80},{6,96},{7,112},{8,128},{9... | collective-permute-start | bytes 98312 | tf_op jit(solution)/shard_map/ppermute | solution.py:167
  26.1 26.3 %all-to-all-start.1 = ((f32[8,16,512]{2,1,0:T(8,128)}), f32[8,16,512]{2,1,0:T(8,128)S(1)}, u32[]{:S(2)}, u32[]{:S(2)}) async-start(f32[8,16,512]{2,1,0:T(8,128)} %broadcast_in_dim.131), calls=%async_computation.1 | async-start | bytes 524288 | tf_op jit(solution)/shard_map/all_to_all | solution.py:151
  52.3 1.5 collective-permute-start.1
  90.0 20.2 %all-to-all-start.4 = ((f32[16,32,256]{2,1,0:T(8,128)}), f32[16,32,256]{2,1,0:T(8,128)S(1)}, u32[]{:S(2)}, u32[]{:S(2)}) async-start(f32[16,32,256]{2,1,0:T(8,128)} %broadcast_in_dim.139), calls=%async_computation.4 | async-start | bytes 1048576 | tf_op jit(solution)/shard_map/all_to_all | solution.py:151
  93.7 5.6 %collective-permute-start.2 = (f32[2,16,512]{2,1,0:T(8,128)S(1)}, f32[2,16,512]{2,1,0:T(8,128)S(1)}, u32[]{:S(2)}, u32[]{:S(2)}) collective-permute-start(f32[2,16,512]{2,1,0:T(8,128)S(1)} %pad_maximum_fusion.20), channel_id=1, source_target_pairs={{0,0},{1,16},{2,32},{3,48},{4,64},{5,80},{6,96},{7,112},{8,128},{9... | collective-permute-start | bytes 196616 | tf_op jit(solution)/shard_map/ppermute | solution.py:167
  110.2 8.1 %copy-start.8 = (f32[16,32,256]{2,1,0:T(8,128)}, f32[16,32,256]{2,1,0:T(8,128)S(1)}, u32[]{:S(2)}) copy-start(f32[16,32,256]{2,1,0:T(8,128)S(1)} %all-to-all-done.4.pieces_ref) | copy-start | bytes 1572868
  111.2 28.0 %all-to-all-start.3 = ((f32[8,2,16,512]{3,2,1,0:T(8,128)}), f32[8,2,16,512]{3,2,1,0:T(8,128)S(1)}, u32[]{:S(2)}, u32[]{:S(2)}) async-start(f32[8,2,16,512]{3,2,1,0:T(8,128)} %broadcast_in_dim.138), calls=%async_computation.3 | async-start | bytes 1048576 | tf_op jit(solution)/shard_map/all_to_all | solution.py:151
  119.6 20.7 %copy-start.1 = (f32[256,512]{1,0:T(8,128)}, f32[256,512]{1,0:T(8,128)S(1)}, u32[]{:S(2)}) copy-start(f32[256,512]{1,0:T(8,128)S(1)} %reshape.224) | copy-start | bytes 1572868
  119.8 21.6 %copy-start.22 = (f32[256,256]{0,1:T(8,128)S(1)}, f32[256,256]{0,1:T(8,128)}, u32[]{:S(2)}) copy-start(f32[256,256]{0,1:T(8,128)} %copy.140) | copy-start | bytes 786436
  142.2 9.7 %copy-start.21 = (f32[256,256]{1,0:T(8,128)S(1)}, f32[256,256]{1,0:T(8,128)}, u32[]{:S(2)}) copy-start(f32[256,256]{1,0:T(8,128)} %get-tuple-element.51) | copy-start | bytes 786436
  142.4 10.4 %slice-start = ((f32[16,32,256]{2,1,0:T(8,128)}), f32[16,16,256]{2,1,0:T(8,128)S(1)}, s32[]{:S(2)}) async-start(f32[16,32,256]{2,1,0:T(8,128)} %copy-done.8), calls=%async_computation.11 | async-start | bytes 524288 | tf_op jit(solution)/shard_map/slice | solution.py:294
  142.4 1.3 collective-permute-start.4
  144.6 25.0 %all-to-all-start.5 = ((f32[8,64,256]{2,1,0:T(8,128)}), f32[8,64,256]{2,1,0:T(8,128)S(1)}, u32[]{:S(2)}, u32[]{:S(2)}) async-start(f32[8,64,256]{2,1,0:T(8,128)} %broadcast_in_dim.142), calls=%async_computation.5 | async-start | bytes 1048576 | tf_op jit(solution)/shard_map/all_to_all | solution.py:151
  151.8 31.3 %collective-permute-start.3 = (f32[8,2,16,512]{3,2,1,0:T(8,128)S(1)}, f32[8,2,16,512]{3,2,1,0:T(8,128)}, u32[]{:S(2)}, u32[]{:S(2)}) collective-permute-start(f32[8,2,16,512]{3,2,1,0:T(8,128)S(1)} %all-to-all-done.3), channel_id=1, source_target_pairs={{0,1},{1,0},{2,3},{3,2},{4,5},{5,4},{6,7},{7,6},{8,9},{9,8},{10,11... | collective-permute-start | bytes 1572872 | tf_op jit(solution)/shard_map/ppermute | solution.py:171
  151.9 60.9 %copy-start.29 = (pred[512]{0:T(512)(128)(4,1)}, pred[512]{0:T(512)(128)(4,1)S(1)}, u32[]{:S(2)}) copy-start(pred[512]{0:T(512)(128)(4,1)S(1)} %broadcast_compare_fusion) | copy-start | bytes 1540
  169.7 35.7 %copy-start.24 = (f32[64,256]{1,0:T(8,128)}, f32[64,256]{1,0:T(8,128)S(1)}, u32[]{:S(2)}) copy-start(f32[64,256]{1,0:T(8,128)S(1)} %reduce_sum.56) | copy-start | bytes 196612
  170.9 29.2 %all-to-all-start.6 = ((f32[16,80,256]{2,1,0:T(8,128)}), f32[16,80,256]{2,1,0:T(8,128)S(1)}, u32[]{:S(2)}, u32[]{:S(2)}) async-start(f32[16,80,256]{2,1,0:T(8,128)} %broadcast_in_dim.143), calls=%async_computation.6 | async-start | bytes 2621440 | tf_op jit(solution)/shard_map/all_to_all | solution.py:151
  184.5 3.2 copy-start.15
  185.6 3.7 %copy-start = (f32[256,256]{1,0:T(8,128)S(1)}, f32[256,256]{1,0:T(8,128)}, u32[]{:S(2)}) copy-start(f32[256,256]{1,0:T(8,128)} %get-tuple-element.20) | copy-start | bytes 786436
  206.3 0.8 slice-start.1
  206.3 2.5 copy-start.4
  207.1 1.4 copy-start.20
  208.4 2.0 copy-start.6
  210.4 2.0 copy-start.7
  210.4 2.4 copy-start.13
  212.8 1.3 copy-start.10
  243.4 5.5 %copy-start.2 = (f32[256,512]{1,0:T(8,128)S(1)}, f32[256,512]{1,0:T(8,128)}, u32[]{:S(2)}) copy-start(f32[256,512]{1,0:T(8,128)} %copy-done.1) | copy-start | bytes 1572868
  244.4 5.6 %copy-start.11 = (f32[256,256]{1,0:T(8,128)S(1)}, f32[256,256]{1,0:T(8,128)}, u32[]{:S(2)}) copy-start(f32[256,256]{1,0:T(8,128)} %copy-done.10) | copy-start | bytes 786436
  245.2 19.5 %all-to-all-start.8 = ((f32[16,32,256]{2,1,0:T(8,128)}), f32[16,32,256]{2,1,0:T(8,128)S(1)}, u32[]{:S(2)}, u32[]{:S(2)}) async-start(f32[16,32,256]{2,1,0:T(8,128)} %broadcast_in_dim.147), calls=%async_computation.8 | async-start | bytes 1048576 | tf_op jit(solution)/shard_map/all_to_all | solution.py:151
  252.4 38.7 %copy-start.14 = (f32[256,512]{0,1:T(8,128)S(1)}, f32[256,512]{0,1:T(8,128)}, u32[]{:S(2)}) copy-start(f32[256,512]{0,1:T(8,128)} %fusion.5) | copy-start | bytes 1572868
  264.7 0.8 copy-start.12
  286.4 7.1 %collective-permute-start.5 = (f32[16,512]{1,0:T(8,128)S(1)}, f32[16,512]{1,0:T(8,128)S(1)}, u32[]{:S(2)}, u32[]{:S(2)}) collective-permute-start(f32[16,512]{1,0:T(8,128)S(1)} %convolution_add_fusion.1), channel_id=1, source_target_pairs={{0,0},{1,16},{2,32},{3,48},{4,64},{5,80},{6,96},{7,112},{8,128},{9... | collective-permute-start | bytes 98312 | tf_op jit(solution)/shard_map/ppermute | solution.py:167
  292.2 1.3 collective-permute-start.6
  294.3 24.2 %all-to-all-start.9 = ((f32[8,24,512]{2,1,0:T(8,128)}), f32[8,24,512]{2,1,0:T(8,128)S(1)}, u32[]{:S(2)}, u32[]{:S(2)}) async-start(f32[8,24,512]{2,1,0:T(8,128)} %broadcast_in_dim.150), calls=%async_computation.9 | async-start | bytes 786432 | tf_op jit(solution)/shard_map/all_to_all | solution.py:151
  305.0 21.1 %copy-start.18 = (f32[256,256]{1,0:T(8,128)S(1)}, f32[256,256]{1,0:T(8,128)}, u32[]{:S(2)}) copy-start(f32[256,256]{1,0:T(8,128)} %get-tuple-element.21) | copy-start | bytes 786436
  318.5 8.4 %copy-start.25 = (f32[256,256]{1,0:T(8,128)S(1)}, f32[256,256]{1,0:T(8,128)}, u32[]{:S(2)}) copy-start(f32[256,256]{1,0:T(8,128)} %get-tuple-element.22) | copy-start | bytes 786436
  318.5 9.3 %collective-permute-start.7 = (f32[8,16,512]{2,1,0:T(8,128)S(1)}, f32[8,16,512]{2,1,0:T(8,128)S(1)}, u32[]{:S(2)}, u32[]{:S(2)}) collective-permute-start(f32[8,16,512]{2,1,0:T(8,128)S(1)} %slice.169), channel_id=1, source_target_pairs={{0,1},{1,0},{2,3},{3,2},{4,5},{5,4},{6,7},{7,6},{8,9},{9,8},{10,11... | collective-permute-start | bytes 786440 | tf_op jit(solution)/shard_map/ppermute | solution.py:171
  319.7 19.5 %all-to-all-start.10 = ((f32[16,48,256]{2,1,0:T(8,128)}), f32[16,48,256]{2,1,0:T(8,128)S(1)}, u32[]{:S(2)}, u32[]{:S(2)}) async-start(f32[16,48,256]{2,1,0:T(8,128)} %broadcast_in_dim.151), calls=%async_computation.10 | async-start | bytes 1572864 | tf_op jit(solution)/shard_map/all_to_all | solution.py:151
  327.8 0.9 copy-start.3
  340.0 1.2 copy-start.16
  340.0 1.2 copy-start.17
  340.7 1.3 copy-start.5
  340.7 1.3 copy-start.19
  340.7 1.4 copy-start.26
  340.7 1.4 copy-start.27
  340.7 1.5 copy-start.28
  340.7 1.5 copy-start.30
  340.7 1.5 copy-start.31
  340.8 1.5 copy-start.32
  340.8 1.5 copy-start.33

commit v4 on v3

--- a/solution.py
+++ b/solution.py
@@ -216,33 +216,39 @@
         x_piece = lax.dynamic_slice_in_dim(x_rows, col_index * part, part, 0)
         gram_part = product(x_piece, x_rows, NT, highest)
         top_part = jnp.where(row_index == panel + 1, x_piece[:, :width], 0.0)
-        shared = [gram_part, top_part, c_own.reshape(2 * part, width)]
+        first = jnp.concatenate([gram_part, top_part])
+        rest = [c_own.reshape(2 * part, width)]
         if panel == 0:
-            shared.append(x_own.reshape(2 * part, width))
-        shared = jnp.concatenate(shared)
-        merged = jnp.concatenate(
-            [
-                jnp.broadcast_to(shared, (devices, *shared.shape)),
-                u_part.reshape(devices, 2 * part, width),
-            ],
-            axis=1,
-        )
-        merged = exchange(merged, "row")
-        sums = copied(jnp.sum(merged[:, : 2 * part], axis=0), COL)
-        pieces = sums
-        c_cols = merged[:, 2 * part : 4 * part].reshape(width, local)
-        if panel == 0:
-            x_cols = merged[:, 4 * part : 6 * part].reshape(width, local)
+            rest.append(x_own.reshape(2 * part, width))
+        rest = jnp.concatenate(rest)
+        each = u_part.reshape(devices, 2 * part, width)
+
+        def spread_out(lines):
+            return jnp.broadcast_to(lines, (devices, *lines.shape))
+
+        if last:
+            sums = jnp.sum(exchange(spread_out(first), "row"), axis=0)
+        else:
+            lines = spread_out(jnp.concatenate([first, rest]))
+            merged = exchange(jnp.concatenate([lines, each], axis=1), "row")
+            sums = jnp.sum(merged[:, : 2 * part], axis=0)
+            merged = merged[:, 2 * part :]
+        pieces = copied(sums, COL)
+        if last:
+            merged = exchange(jnp.concatenate([spread_out(rest), each], axis=1), "row")
+            factors = factor(pieces)
+            merged, (upper, lower, core) = lax.optimization_barrier((merged, factors))
         u_own = jnp.sum(merged[:, -2 * part :], axis=0).reshape(part, local)
         u_own = jnp.where(below_cols, u_own, 0.0)
-        if last:
-            upper, lower, core = factor(pieces)
-        else:
+        if not last:
             pair = transposed(jnp.stack([u_own, c_own]))
             pair = copied(pair, COL[0])
             factors = factor(pieces)
             pair, (upper, lower, core) = lax.optimization_barrier((pair, factors))
             u_rows, c_rows = join(both_cores(pair))
+        c_cols = merged[:, : 2 * part].reshape(width, local)
+        if panel == 0:
+            x_cols = merged[:, 2 * part : 4 * part].reshape(width, local)
 
         def with_top(x, index):
             head = jnp.where(index == panel + 1, lower, 0.0)

time: 352 us -> 361 us (1.026)
  blocking collectives: 59.4 us -> 32.5 us
  starting transfers between devices: 79.2 us -> 94.4 us
  waiting for transfers between devices: 101 us -> 107 us
  local copies, waits for them, and re-layouts: 32.4 us -> 37.7 us
  other arithmetic: 9.1 us -> 13.8 us
    all_to_all x2 -> x1, blocking collectives: 59.4 us -> 32.5 us  [exchange(): return lax.all_to_all(value, axis, 0, 0, tiled=True)]
    all_to_all x9 -> x11, starting transfers between devices: 69.1 us -> 85.5 us  [exchange(): return lax.all_to_all(value, axis, 0, 0, tiled=True)]
    all_to_all x9 -> x11, waiting for transfers between devices: 91.2 us -> 97.9 us  [exchange(): return lax.all_to_all(value, axis, 0, 0, tiled=True)]
  transfers between devices with their start and end apart: 17 -> 19, of which waited for: 13 -> 14; matrix products, arithmetic and copies ran while one was open for 8% -> 10% of each run, Pallas kernels for 6% -> 11%
where the time goes in v4:
time: 361 us; the launch traced here: 354 us
  waiting for transfers between devices  107 us (30%)
  starting transfers between devices  94.4 us (26%)
  Pallas kernels  38.1 us (11%)
  local copies, waits for them, and re-layouts  37.7 us (10%)
  blocking collectives  32.5 us (9%)
  matrix products  28.6 us (8%)
  other arithmetic  13.8 us (4%)
    all_to_all x11, waiting for transfers between devices, exchange(): return lax.all_to_all(value, axis, 0, 0, tiled=True)  97.9 us
    all_to_all x11, starting transfers between devices, exchange(): return lax.all_to_all(value, axis, 0, 0, tiled=True)  85.5 us
    pallas_call x2, Pallas kernels, factor(): pl.pallas_call(functools.partial(factor_kernel, b=32), out_shape=(square,...  38.1 us
    all_to_all x1, blocking collectives, exchange(): return lax.all_to_all(value, axis, 0, 0, tiled=True)  32.5 us
    dot_general x30, matrix products, product(): lax.dot_general(left, right, (dims, ((), ())), precision=precision, prefe...  28.6 us
    ppermute x3, starting transfers between devices, transposed(): return lax.ppermute(row_major(value), ('row', *COL), pairs)  8.69 us
    broadcast_in_dim x8, local copies, waits for them, and re-layouts, copied(): copies = jnp.broadcast_to(value, (lax.axis_size(axis), *value.shape))  7.28 us
  transfers between devices with their start and end apart: 19, of which 14 were waited for; matrix products, arithmetic and copies ran while one was open for 10% of the time, Pallas kernels for 11%

profile of v4, /device:TPU:2, one launch (start us, length us, event | category | flops | bytes accessed | tf_op | source)
XLA Modules:
  0.0 353.9 jit_solution(8272738953024809662)
XLA Ops:
  0.0 1.3 slice.109
  1.3 1.2 reshape.217
  2.5 7.5 %all-to-all-start = ((f32[16,16,512]{2,1,0:T(8,128)}), f32[16,16,512]{2,1,0:T(8,128)S(1)}, u32[]{:S(2)}, u32[]{:S(2)}) async-start(f32[16,16,512]{2,1,0:T(8,128)} %reshape.217), calls=%async_computation | async-start | bytes 1048576 | tf_op jit(solution)/shard_map/all_to_all | solution.py:151
  10.0 10.2 %all-to-all-done = f32[16,16,512]{2,1,0:T(8,128)S(1)} async-done(((f32[16,16,512]{2,1,0:T(8,128)}), f32[16,16,512]{2,1,0:T(8,128)S(1)}, u32[]{:S(2)}, u32[]{:S(2)}) %all-to-all-start) | async-done | bytes 524320 | tf_op jit(solution)/shard_map/all_to_all | solution.py:151
  20.2 1.9 collective-permute-start
  22.1 3.3 collective-permute-done
  26.2 15.8 %all-to-all-start.1 = ((f32[8,16,512]{2,1,0:T(8,128)}), f32[8,16,512]{2,1,0:T(8,128)S(1)}, u32[]{:S(2)}, u32[]{:S(2)}) async-start(f32[8,16,512]{2,1,0:T(8,128)} %broadcast_in_dim.133), calls=%async_computation.1 | async-start | bytes 524288 | tf_op jit(solution)/shard_map/all_to_all | solution.py:151
  42.1 10.3 %all-to-all-done.1 = f32[8,16,512]{2,1,0:T(8,128)S(1)} async-done(((f32[8,16,512]{2,1,0:T(8,128)}), f32[8,16,512]{2,1,0:T(8,128)S(1)}, u32[]{:S(2)}, u32[]{:S(2)}) %all-to-all-start.1) | async-done | bytes 262176 | tf_op jit(solution)/shard_map/all_to_all | solution.py:151
  52.5 1.5 collective-permute-done.1
  55.9 32.5 %all_to_all.60 = f32[16,128,256]{2,1,0:T(8,128)S(1)} all-to-all(f32[16,128,256]{2,1,0:T(8,128)S(1)} %pad_maximum_fusion), channel_id=1, replica_groups=mesh['row'=16,'col_0'=8,'col_1'=2] {'row'}, dimensions={0} | all-to-all | bytes 4194304 | tf_op jit(solution)/shard_map/all_to_all | solution.py:151
  90.1 3.6 %all-to-all-start.4 = ((f32[16,32,256]{2,1,0:T(8,128)}), f32[16,32,256]{2,1,0:T(8,128)S(1)}, u32[]{:S(2)}, u32[]{:S(2)}) async-start(f32[16,32,256]{2,1,0:T(8,128)} %broadcast_in_dim.142), calls=%async_computation.4 | async-start | bytes 1048576 | tf_op jit(solution)/shard_map/all_to_all | solution.py:151
  93.8 3.3 collective-permute-start.2
  97.0 2.3 collective-permute-done.2
  99.3 11.0 %all-to-all-done.4.pieces_ref = f32[16,32,256]{2,1,0:T(8,128)S(1)} async-done(((f32[16,32,256]{2,1,0:T(8,128)}), f32[16,32,256]{2,1,0:T(8,128)S(1)}, u32[]{:S(2)}, u32[]{:S(2)}) %all-to-all-start.4) | async-done | bytes 524320 | tf_op jit(solution)/shard_map/all_to_all | solution.py:151
  111.3 5.5 %all-to-all-start.3 = ((f32[8,2,16,512]{3,2,1,0:T(8,128)}), f32[8,2,16,512]{3,2,1,0:T(8,128)S(1)}, u32[]{:S(2)}, u32[]{:S(2)}) async-start(f32[8,2,16,512]{3,2,1,0:T(8,128)} %broadcast_in_dim.141), calls=%async_computation.3 | async-start | bytes 1048576 | tf_op jit(solution)/shard_map/all_to_all | solution.py:151
  118.4 1.2 reshape.225
  120.5 1.1 copy.140
  121.7 1.1 copy.141
  122.9 19.1 %factor.2 = (f32[256,256]{1,0:T(8,128)}, f32[256,256]{1,0:T(8,128)}, f32[256,256]{1,0:T(8,128)}) custom-call(f32[16,32,256]{2,1,0:T(8,128)} %copy-done.12), custom_call_target="tpu_custom_call" | custom-call | tf_op jit(solution)/shard_map/factor/pallas_call | solution.py:138
  142.0 1.8 copy.97
  143.7 0.9 convolution_add_fusion.2
  144.9 1.7 select_add_fusion.1
  147.0 1.2 collective-permute-done.3
  149.1 7.2 %all-to-all-start.5 = ((f32[8,64,256]{2,1,0:T(8,128)}), f32[8,64,256]{2,1,0:T(8,128)}, u32[]{:S(2)}, u32[]{:S(2)}) async-start(f32[8,64,256]{2,1,0:T(8,128)} %broadcast_in_dim.145), calls=%async_computation.5 | async-start | bytes 1048576 | tf_op jit(solution)/shard_map/all_to_all | solution.py:151
  157.8 16.4 %all-to-all-done.5 = f32[8,64,256]{2,1,0:T(8,128)} async-done(((f32[8,64,256]{2,1,0:T(8,128)}), f32[8,64,256]{2,1,0:T(8,128)}, u32[]{:S(2)}, u32[]{:S(2)}) %all-to-all-start.5) | async-done | bytes 524320 | tf_op jit(solution)/shard_map/all_to_all | solution.py:151
  174.2 1.1 reduce_sum.56
  175.3 1.2 broadcast_in_dim.146
  176.5 10.4 %all-to-all-start.6 = ((f32[16,80,256]{2,1,0:T(8,128)}), f32[16,80,256]{2,1,0:T(8,128)}, u32[]{:S(2)}, u32[]{:S(2)}) async-start(f32[16,80,256]{2,1,0:T(8,128)} %broadcast_in_dim.146), calls=%async_computation.6 | async-start | bytes 2621440 | tf_op jit(solution)/shard_map/all_to_all | solution.py:151
  187.7 1.1 select_bitcast_fusion.1
  189.9 1.0 copy.113
  190.9 1.4 convolution_add_fusion
  192.4 1.4 fusion.88
  193.8 12.1 %all-to-all-done.6 = f32[16,80,256]{2,1,0:T(8,128)} async-done(((f32[16,80,256]{2,1,0:T(8,128)}), f32[16,80,256]{2,1,0:T(8,128)}, u32[]{:S(2)}, u32[]{:S(2)}) %all-to-all-start.6) | async-done | bytes 1310752 | tf_op jit(solution)/shard_map/all_to_all | solution.py:151
  205.9 2.0 fusion.77
  208.5 1.9 slice.157
  210.5 2.0 reshape.228
  212.5 2.5 fusion.86
  215.1 1.4 fusion.87
  221.8 6.6 %all-to-all-start.8 = ((f32[16,32,256]{2,1,0:T(8,128)}), f32[16,32,256]{2,1,0:T(8,128)}, u32[]{:S(2)}, u32[]{:S(2)}) async-start(f32[16,32,256]{2,1,0:T(8,128)} %broadcast_in_dim.150), calls=%async_computation.8 | async-start | bytes 1048576 | tf_op jit(solution)/shard_map/all_to_all | solution.py:151
  228.3 1.5 convolution_subtract_fusion.7
  230.7 3.0 convolution_subtract_fusion.1
  233.7 4.2 %all-to-all-done.8 = f32[16,32,256]{2,1,0:T(8,128)} async-done(((f32[16,32,256]{2,1,0:T(8,128)}), f32[16,32,256]{2,1,0:T(8,128)}, u32[]{:S(2)}, u32[]{:S(2)}) %all-to-all-start.8) | async-done | bytes 524320 | tf_op jit(solution)/shard_map/all_to_all | solution.py:151
  237.8 1.1 reduce_sum.57
  239.8 4.4 %all-to-all-start.9 = ((f32[16,32,256]{2,1,0:T(8,128)}), f32[16,32,256]{2,1,0:T(8,128)}, u32[]{:S(2)}, u32[]{:S(2)}) async-start(f32[16,32,256]{2,1,0:T(8,128)} %broadcast_in_dim.151), calls=%async_computation.9 | async-start | bytes 1048576 | tf_op jit(solution)/shard_map/all_to_all | solution.py:151
  244.2 2.7 fusion.89
  246.9 1.1 reshape.233
  248.8 1.3 fusion.6
  250.1 1.1 pad_maximum_fusion.3
  251.2 8.9 %all-to-all-done.9.pieces_ref = f32[16,32,256]{2,1,0:T(8,128)} async-done(((f32[16,32,256]{2,1,0:T(8,128)}), f32[16,32,256]{2,1,0:T(8,128)}, u32[]{:S(2)}, u32[]{:S(2)}) %all-to-all-start.9) | async-done | bytes 524320 | tf_op jit(solution)/shard_map/all_to_all | solution.py:151
  260.1 5.7 %all-to-all-start.7 = ((f32[16,64,256]{2,1,0:T(8,128)}), f32[16,64,256]{2,1,0:T(8,128)}, u32[]{:S(2)}, u32[]{:S(2)}) async-start(f32[16,64,256]{2,1,0:T(8,128)} %pad_maximum_fusion.3), calls=%async_computation.7 | async-start | bytes 2097152 | tf_op jit(solution)/shard_map/all_to_all | solution.py:151
  266.0 1.4 fusion.5
  267.4 19.0 %factor.3 = (f32[256,256]{1,0:T(8,128)}, f32[256,256]{1,0:T(8,128)}, f32[256,256]{1,0:T(8,128)}) custom-call(f32[16,32,256]{2,1,0:T(8,128)} %all-to-all-done.9.pieces_ref), custom_call_target="tpu_custom_call" | custom-call | tf_op jit(solution)/shard_map/factor/pallas_call | solution.py:138
  286.4 1.1 copy.120
  287.5 1.3 slice_reduce_fusion.2
  288.9 1.0 convolution_add_fusion.1
  289.9 3.5 collective-permute-start.5
  294.6 1.2 collective-permute-done.6
  296.6 10.7 %all-to-all-start.10 = ((f32[8,24,512]{2,1,0:T(8,128)}), f32[8,24,512]{2,1,0:T(8,128)S(1)}, u32[]{:S(2)}, u32[]{:S(2)}) async-start(f32[8,24,512]{2,1,0:T(8,128)} %broadcast_in_dim.154), calls=%async_computation.10 | async-start | bytes 786432 | tf_op jit(solution)/shard_map/all_to_all | solution.py:151
  308.0 14.3 %all-to-all-done.10 = f32[8,24,512]{2,1,0:T(8,128)S(1)} async-done(((f32[8,24,512]{2,1,0:T(8,128)}), f32[8,24,512]{2,1,0:T(8,128)S(1)}, u32[]{:S(2)}, u32[]{:S(2)}) %all-to-all-start.10) | async-done | bytes 393248 | tf_op jit(solution)/shard_map/all_to_all | solution.py:151
  322.4 1.0 broadcast_in_dim.155
  323.4 8.1 %all-to-all-start.11 = ((f32[16,48,256]{2,1,0:T(8,128)}), f32[16,48,256]{2,1,0:T(8,128)S(1)}, u32[]{:S(2)}, u32[]{:S(2)}) async-start(f32[16,48,256]{2,1,0:T(8,128)} %broadcast_in_dim.155), calls=%async_computation.11 | async-start | bytes 1572864 | tf_op jit(solution)/shard_map/all_to_all | solution.py:151
  334.6 10.7 %all-to-all-done.11 = f32[16,48,256]{2,1,0:T(8,128)S(1)} async-done(((f32[16,48,256]{2,1,0:T(8,128)}), f32[16,48,256]{2,1,0:T(8,128)S(1)}, u32[]{:S(2)}, u32[]{:S(2)}) %all-to-all-start.11) | async-done | bytes 786464 | tf_op jit(solution)/shard_map/all_to_all | solution.py:151
  348.3 2.5 fusion.3
  350.8 2.8 reshape.242
  (200 shorter events, 29.9 us)
Async XLA Ops:
  0.0 41.9 %copy-start.13 = (f32[2,256,2,256]{3,2,1,0:T(2,128)S(1)}, f32[2,256,2,256]{3,2,1,0:T(2,128)}, u32[]{:S(2)}) copy-start(f32[2,256,2,256]{3,2,1,0:T(2,128)} %param.1) | copy-start | bytes 3145732
  2.5 17.6 %all-to-all-start = ((f32[16,16,512]{2,1,0:T(8,128)}), f32[16,16,512]{2,1,0:T(8,128)S(1)}, u32[]{:S(2)}, u32[]{:S(2)}) async-start(f32[16,16,512]{2,1,0:T(8,128)} %reshape.217), calls=%async_computation | async-start | bytes 1048576 | tf_op jit(solution)/shard_map/all_to_all | solution.py:151
  10.0 133.7 %copy-start.35 = (pred[512]{0:T(512)(128)(4,1)}, pred[512]{0:T(512)(128)(4,1)S(1)}, u32[]{:S(2)}) copy-start(pred[512]{0:T(512)(128)(4,1)S(1)} %broadcast_compare_fusion.3) | copy-start | bytes 1540
  20.2 33.8 %copy-start.28 = (f32[16,16,512]{2,1,0:T(8,128)}, f32[16,16,512]{2,1,0:T(8,128)S(1)}, u32[]{:S(2)}) copy-start(f32[16,16,512]{2,1,0:T(8,128)S(1)} %all-to-all-done) | copy-start | bytes 1572868
  20.2 5.2 %collective-permute-start = (f32[16,512]{1,0:T(8,128)S(1)}, f32[16,512]{1,0:T(8,128)S(1)}, u32[]{:S(2)}, u32[]{:S(2)}) collective-permute-start(f32[16,512]{1,0:T(8,128)S(1)} %bitcast_select_fusion), channel_id=1, source_target_pairs={{0,0},{1,16},{2,32},{3,48},{4,64},{5,80},{6,96},{7,112},{8,128},{9... | collective-permute-start | bytes 98312 | tf_op jit(solution)/shard_map/ppermute | solution.py:167
  26.2 26.3 %all-to-all-start.1 = ((f32[8,16,512]{2,1,0:T(8,128)}), f32[8,16,512]{2,1,0:T(8,128)S(1)}, u32[]{:S(2)}, u32[]{:S(2)}) async-start(f32[8,16,512]{2,1,0:T(8,128)} %broadcast_in_dim.133), calls=%async_computation.1 | async-start | bytes 524288 | tf_op jit(solution)/shard_map/all_to_all | solution.py:151
  52.4 1.5 collective-permute-start.1
  90.1 20.2 %all-to-all-start.4 = ((f32[16,32,256]{2,1,0:T(8,128)}), f32[16,32,256]{2,1,0:T(8,128)S(1)}, u32[]{:S(2)}, u32[]{:S(2)}) async-start(f32[16,32,256]{2,1,0:T(8,128)} %broadcast_in_dim.142), calls=%async_computation.4 | async-start | bytes 1048576 | tf_op jit(solution)/shard_map/all_to_all | solution.py:151
  93.8 5.6 %collective-permute-start.2 = (f32[2,16,512]{2,1,0:T(8,128)S(1)}, f32[2,16,512]{2,1,0:T(8,128)S(1)}, u32[]{:S(2)}, u32[]{:S(2)}) collective-permute-start(f32[2,16,512]{2,1,0:T(8,128)S(1)} %pad_maximum_fusion.20), channel_id=1, source_target_pairs={{0,0},{1,16},{2,32},{3,48},{4,64},{5,80},{6,96},{7,112},{8,128},{9... | collective-permute-start | bytes 196616 | tf_op jit(solution)/shard_map/ppermute | solution.py:167
  110.3 9.3 %copy-start.12 = (f32[16,32,256]{2,1,0:T(8,128)}, f32[16,32,256]{2,1,0:T(8,128)S(1)}, u32[]{:S(2)}) copy-start(f32[16,32,256]{2,1,0:T(8,128)S(1)} %all-to-all-done.4.pieces_ref) | copy-start | bytes 1572868
  111.3 30.7 %all-to-all-start.3 = ((f32[8,2,16,512]{3,2,1,0:T(8,128)}), f32[8,2,16,512]{3,2,1,0:T(8,128)S(1)}, u32[]{:S(2)}, u32[]{:S(2)}) async-start(f32[8,2,16,512]{3,2,1,0:T(8,128)} %broadcast_in_dim.141), calls=%async_computation.3 | async-start | bytes 1048576 | tf_op jit(solution)/shard_map/all_to_all | solution.py:151
  120.5 24.4 %copy-start.27 = (f32[256,256]{0,1:T(8,128)S(1)}, f32[256,256]{0,1:T(8,128)}, u32[]{:S(2)}) copy-start(f32[256,256]{0,1:T(8,128)} %copy.142) | copy-start | bytes 786436
  144.8 12.7 %copy-start.26 = (f32[256,256]{1,0:T(8,128)S(1)}, f32[256,256]{1,0:T(8,128)}, u32[]{:S(2)}) copy-start(f32[256,256]{1,0:T(8,128)} %get-tuple-element.58) | copy-start | bytes 786436
  146.6 11.0 %slice-start = ((f32[16,32,256]{2,1,0:T(8,128)}), f32[16,16,256]{2,1,0:T(8,128)S(1)}, s32[]{:S(2)}) async-start(f32[16,32,256]{2,1,0:T(8,128)} %copy-done.12), calls=%async_computation.12 | async-start | bytes 524288 | tf_op jit(solution)/shard_map/slice | solution.py:300
  146.9 1.3 collective-permute-start.3
  149.1 25.1 %all-to-all-start.5 = ((f32[8,64,256]{2,1,0:T(8,128)}), f32[8,64,256]{2,1,0:T(8,128)}, u32[]{:S(2)}, u32[]{:S(2)}) async-start(f32[8,64,256]{2,1,0:T(8,128)} %broadcast_in_dim.145), calls=%async_computation.5 | async-start | bytes 1048576 | tf_op jit(solution)/shard_map/all_to_all | solution.py:151
  156.3 31.4 %collective-permute-start.4 = (f32[8,2,16,512]{3,2,1,0:T(8,128)S(1)}, f32[8,2,16,512]{3,2,1,0:T(8,128)}, u32[]{:S(2)}, u32[]{:S(2)}) collective-permute-start(f32[8,2,16,512]{3,2,1,0:T(8,128)S(1)} %all-to-all-done.3), channel_id=1, source_target_pairs={{0,1},{1,0},{2,3},{3,2},{4,5},{5,4},{6,7},{7,6},{8,9},{9,8},{10,11... | collective-permute-start | bytes 1572872 | tf_op jit(solution)/shard_map/ppermute | solution.py:171
  157.5 59.9 %copy-start.38 = (pred[512]{0:T(512)(128)(4,1)}, pred[512]{0:T(512)(128)(4,1)S(1)}, u32[]{:S(2)}) copy-start(pred[512]{0:T(512)(128)(4,1)S(1)} %get-tuple-element.69) | copy-start | bytes 1540
  175.3 18.5 %copy-start.29 = (f32[64,256]{1,0:T(8,128)}, f32[64,256]{1,0:T(8,128)S(1)}, u32[]{:S(2)}) copy-start(f32[64,256]{1,0:T(8,128)S(1)} %reduce_sum.56) | copy-start | bytes 196612
  175.3 11.6 %copy-start.22 = (f32[256,256]{1,0:T(8,128)S(1)}, f32[256,256]{1,0:T(8,128)}, u32[]{:S(2)}) copy-start(f32[256,256]{1,0:T(8,128)} %get-tuple-element.25) | copy-start | bytes 786436
  176.5 29.4 %all-to-all-start.6 = ((f32[16,80,256]{2,1,0:T(8,128)}), f32[16,80,256]{2,1,0:T(8,128)}, u32[]{:S(2)}, u32[]{:S(2)}) async-start(f32[16,80,256]{2,1,0:T(8,128)} %broadcast_in_dim.146), calls=%async_computation.6 | async-start | bytes 2621440 | tf_op jit(solution)/shard_map/all_to_all | solution.py:151
  189.0 1.9 copy-start.19
  189.0 3.3 copy-start
  208.5 8.0 %copy-start.9 = (f32[256,256]{1,0:T(8,128)S(1)}, f32[256,256]{1,0:T(8,128)}, u32[]{:S(2)}) copy-start(f32[256,256]{1,0:T(8,128)} %bitcast_add_fusion) | copy-start | bytes 786436
  210.5 6.4 %copy-start.7 = (f32[256,256]{0,1:T(8,128)S(1)}, f32[256,256]{0,1:T(8,128)}, u32[]{:S(2)}) copy-start(f32[256,256]{0,1:T(8,128)} %get-tuple-element.64) | copy-start | bytes 786436
  212.5 4.4 %copy-start.16 = (f32[256,512]{0,1:T(8,128)S(1)}, f32[256,512]{0,1:T(8,128)}, u32[]{:S(2)}) copy-start(f32[256,512]{0,1:T(8,128)} %fusion.88) | copy-start | bytes 1572868
  215.0 3.1 copy-start.8
  215.1 3.1 copy-start.10
  215.1 3.1 copy-start.17
  216.8 1.9 copy-start.14
  217.3 0.8 copy-start.3
  221.8 16.1 %all-to-all-start.8 = ((f32[16,32,256]{2,1,0:T(8,128)}), f32[16,32,256]{2,1,0:T(8,128)}, u32[]{:S(2)}, u32[]{:S(2)}) async-start(f32[16,32,256]{2,1,0:T(8,128)} %broadcast_in_dim.150), calls=%async_computation.8 | async-start | bytes 1048576 | tf_op jit(solution)/shard_map/all_to_all | solution.py:151
  228.3 2.3 copy-start.4
  229.9 0.8 copy-start.1
  239.8 8.3 %copy-start.25 = (f32[16,16,256]{2,1,0:T(8,128)S(1)}, f32[16,16,256]{2,1,0:T(8,128)}, u32[]{:S(2)}) copy-start(f32[16,16,256]{2,1,0:T(8,128)} %get-tuple-element.37) | copy-start | bytes 786436
  239.8 20.3 %all-to-all-start.9 = ((f32[16,32,256]{2,1,0:T(8,128)}), f32[16,32,256]{2,1,0:T(8,128)}, u32[]{:S(2)}, u32[]{:S(2)}) async-start(f32[16,32,256]{2,1,0:T(8,128)} %broadcast_in_dim.151), calls=%async_computation.9 | async-start | bytes 1048576 | tf_op jit(solution)/shard_map/all_to_all | solution.py:151
  244.2 4.3 %copy-start.30 = (f32[64,256]{1,0:T(8,128)S(1)}, f32[64,256]{1,0:T(8,128)}, u32[]{:S(2)}) copy-start(f32[64,256]{1,0:T(8,128)} %copy-done.29) | copy-start | bytes 196612
  244.2 4.5 %copy-start.2 = (f32[256,512]{0,1:T(8,128)S(1)}, f32[256,512]{0,1:T(8,128)}, u32[]{:S(2)}) copy-start(f32[256,512]{0,1:T(8,128)} %copy-done.1) | copy-start | bytes 1572868
  244.2 4.6 %slice-start.1 = ((f32[64,256]{1,0:T(8,128)}), f32[16,256]{1,0:T(8,128)S(1)}, s32[]{:S(2)}) async-start(f32[64,256]{1,0:T(8,128)} %copy-done.29), calls=%async_computation.13 | async-start | bytes 32768 | tf_op jit(solution)/shard_map/slice | solution.py:302
  244.2 4.6 %copy-start.36 = (pred[512]{0:T(512)(128)(4,1)S(1)}, pred[512]{0:T(512)(128)(4,1)}, u32[]{:S(2)}) copy-start(pred[512]{0:T(512)(128)(4,1)} %copy-done.35) | copy-start | bytes 1540
  244.2 4.6 %copy-start.37 = (pred[512]{0:T(512)(128)(4,1)S(1)}, pred[512]{0:T(512)(128)(4,1)}, u32[]{:S(2)}) copy-start(pred[512]{0:T(512)(128)(4,1)} %broadcast_compare_fusion.1) | copy-start | bytes 1540
  251.2 14.8 %copy-start.11 = (f32[256,256]{1,0:T(8,128)S(1)}, f32[256,256]{1,0:T(8,128)}, u32[]{:S(2)}) copy-start(f32[256,256]{1,0:T(8,128)} %bitcast_add_fusion) | copy-start | bytes 786436
  251.2 14.8 %copy-start.15 = (f32[256,256]{1,0:T(8,128)S(1)}, f32[256,256]{1,0:T(8,128)}, u32[]{:S(2)}) copy-start(f32[256,256]{1,0:T(8,128)} %copy-done.14) | copy-start | bytes 786436
  260.1 26.3 %all-to-all-start.7 = ((f32[16,64,256]{2,1,0:T(8,128)}), f32[16,64,256]{2,1,0:T(8,128)}, u32[]{:S(2)}, u32[]{:S(2)}) async-start(f32[16,64,256]{2,1,0:T(8,128)} %pad_maximum_fusion.3), calls=%async_computation.7 | async-start | bytes 2097152 | tf_op jit(solution)/shard_map/all_to_all | solution.py:151
  267.4 26.0 %copy-start.18 = (f32[256,512]{0,1:T(8,128)S(1)}, f32[256,512]{0,1:T(8,128)}, u32[]{:S(2)}) copy-start(f32[256,512]{0,1:T(8,128)} %fusion.5) | copy-start | bytes 1572868
  289.9 5.9 %collective-permute-start.5 = (f32[16,512]{1,0:T(8,128)S(1)}, f32[16,512]{1,0:T(8,128)S(1)}, u32[]{:S(2)}, u32[]{:S(2)}) collective-permute-start(f32[16,512]{1,0:T(8,128)S(1)} %convolution_add_fusion.1), channel_id=1, source_target_pairs={{0,0},{1,16},{2,32},{3,48},{4,64},{5,80},{6,96},{7,112},{8,128},{9... | collective-permute-start | bytes 98312 | tf_op jit(solution)/shard_map/ppermute | solution.py:167
  294.5 1.3 collective-permute-start.6
  296.6 35.5 %copy-start.23 = (f32[256,256]{1,0:T(8,128)S(1)}, f32[256,256]{1,0:T(8,128)}, u32[]{:S(2)}) copy-start(f32[256,256]{1,0:T(8,128)} %get-tuple-element.25) | copy-start | bytes 786436
  296.6 25.6 %all-to-all-start.10 = ((f32[8,24,512]{2,1,0:T(8,128)}), f32[8,24,512]{2,1,0:T(8,128)S(1)}, u32[]{:S(2)}, u32[]{:S(2)}) async-start(f32[8,24,512]{2,1,0:T(8,128)} %broadcast_in_dim.154), calls=%async_computation.10 | async-start | bytes 786432 | tf_op jit(solution)/shard_map/all_to_all | solution.py:151
  307.4 25.6 %copy-start.31 = (f32[256,256]{1,0:T(8,128)S(1)}, f32[256,256]{1,0:T(8,128)}, u32[]{:S(2)}) copy-start(f32[256,256]{1,0:T(8,128)} %get-tuple-element.29) | copy-start | bytes 786436
  322.2 11.5 %collective-permute-start.7 = (f32[8,16,512]{2,1,0:T(8,128)S(1)}, f32[8,16,512]{2,1,0:T(8,128)S(1)}, u32[]{:S(2)}, u32[]{:S(2)}) collective-permute-start(f32[8,16,512]{2,1,0:T(8,128)S(1)} %slice.166), channel_id=1, source_target_pairs={{0,1},{1,0},{2,3},{3,2},{4,5},{5,4},{6,7},{7,6},{8,9},{9,8},{10,11... | collective-permute-start | bytes 786440 | tf_op jit(solution)/shard_map/ppermute | solution.py:171
  323.4 21.8 %all-to-all-start.11 = ((f32[16,48,256]{2,1,0:T(8,128)}), f32[16,48,256]{2,1,0:T(8,128)S(1)}, u32[]{:S(2)}, u32[]{:S(2)}) async-start(f32[16,48,256]{2,1,0:T(8,128)} %broadcast_in_dim.155), calls=%async_computation.11 | async-start | bytes 1572864 | tf_op jit(solution)/shard_map/all_to_all | solution.py:151
  332.1 1.8 copy-start.5
  345.9 1.3 copy-start.20
  345.9 1.3 copy-start.21
  346.7 1.3 copy-start.6
  346.7 1.3 copy-start.24
  346.7 1.4 copy-start.32
  346.8 1.4 copy-start.33
  346.8 1.5 copy-start.34
  346.8 1.5 copy-start.39
  346.8 1.5 copy-start.40
  346.8 1.5 copy-start.41
  346.8 1.5 copy-start.42

commit v5 on v4

--- a/solution.py
+++ b/solution.py
@@ -232,7 +232,7 @@
             lines = spread_out(jnp.concatenate([first, rest]))
             merged = exchange(jnp.concatenate([lines, each], axis=1), "row")
             sums = jnp.sum(merged[:, : 2 * part], axis=0)
-            merged = merged[:, 2 * part :]
+            c_cols = merged[:, 2 * part : 4 * part].reshape(width, local)
         pieces = copied(sums, COL)
         if last:
             merged = exchange(jnp.concatenate([spread_out(rest), each], axis=1), "row")
@@ -246,16 +246,17 @@
             factors = factor(pieces)
             pair, (upper, lower, core) = lax.optimization_barrier((pair, factors))
             u_rows, c_rows = join(both_cores(pair))
-        c_cols = merged[:, : 2 * part].reshape(width, local)
+        if last:
+            c_cols = merged[:, : 2 * part].reshape(width, local)
         if panel == 0:
-            x_cols = merged[:, 2 * part : 4 * part].reshape(width, local)
+            x_cols = merged[:, 4 * part : 6 * part].reshape(width, local)
 
         def with_top(x, index):
             head = jnp.where(index == panel + 1, lower, 0.0)
             return jnp.concatenate([x[:, :width] + head, x[:, width:]], axis=1)
 
-        v_cols = with_top(x_cols, col_index)
-        v_rows = with_top(x_rows, row_index)
+        v_cols = row_major(with_top(x_cols, col_index))
+        v_rows = row_major(with_top(x_rows, row_index))
         w_own = u_own + product(lax.dynamic_slice_in_dim(lower, own, part, 0), c_cols)
         parts = [product(w_own, v_cols, NT)]
         if last:
@@ -281,6 +282,7 @@
         middle = 0.5 * product(product(core, inner), core, NT)
         y_cols = product(core, w_cols) - product(middle, v_cols)
         y_rows = product(core, w_rows) - product(middle, v_rows)
+        y_cols, y_rows = row_major(y_cols), row_major(y_rows)
         dense = dense - product(
             jnp.concatenate([y_rows, v_rows]), jnp.concatenate([v_cols, y_cols]), TN
         )

time: 361 us -> 357 us (0.989)
  waiting for transfers between devices: 107 us -> 112 us
  local copies, waits for them, and re-layouts: 37.7 us -> 34 us
    all_to_all x11, waiting for transfers between devices: 97.9 us -> 103 us  [exchange(): return lax.all_to_all(value, axis, 0, 0, tiled=True)]
  transfers between devices with their start and end apart: 19 -> 19, of which waited for: 14 -> 15; matrix products, arithmetic and copies ran while one was open for 10% -> 9% of each run, Pallas kernels for 11% -> 11%
where the time goes in v5:
time: 357 us; the launch traced here: 350 us
  waiting for transfers between devices  112 us (31%)
  starting transfers between devices  95.8 us (27%)
  Pallas kernels  38 us (11%)
  local copies, waits for them, and re-layouts  34 us (10%)
  blocking collectives  32.5 us (9%)
  matrix products  25.8 us (7%)
  other arithmetic  10.6 us (3%)
    all_to_all x11, waiting for transfers between devices, exchange(): return lax.all_to_all(value, axis, 0, 0, tiled=True)  103 us
    all_to_all x11, starting transfers between devices, exchange(): return lax.all_to_all(value, axis, 0, 0, tiled=True)  86 us
    pallas_call x2, Pallas kernels, factor(): pl.pallas_call(functools.partial(factor_kernel, b=32), out_shape=(square,...  38 us
    all_to_all x1, blocking collectives, exchange(): return lax.all_to_all(value, axis, 0, 0, tiled=True)  32.5 us
    dot_general x30, matrix products, product(): lax.dot_general(left, right, (dims, ((), ())), precision=precision, prefe...  25.8 us
    ppermute x3, starting transfers between devices, transposed(): return lax.ppermute(row_major(value), ('row', *COL), pairs)  8.7 us
    broadcast_in_dim x8, local copies, waits for them, and re-layouts, copied(): copies = jnp.broadcast_to(value, (lax.axis_size(axis), *value.shape))  7.2 us
  transfers between devices with their start and end apart: 19, of which 15 were waited for; matrix products, arithmetic and copies ran while one was open for 9% of the time, Pallas kernels for 11%

profile of v5, /device:TPU:2, one launch (start us, length us, event | category | flops | bytes accessed | tf_op | source)
XLA Modules:
  0.0 350.1 jit_solution(2541201723751433368)
XLA Ops:
  0.0 1.3 slice.105
  1.3 1.2 reshape.217
  2.5 7.5 %all-to-all-start = ((f32[16,16,512]{2,1,0:T(8,128)}), f32[16,16,512]{2,1,0:T(8,128)S(1)}, u32[]{:S(2)}, u32[]{:S(2)}) async-start(f32[16,16,512]{2,1,0:T(8,128)} %reshape.217), calls=%async_computation | async-start | bytes 1048576 | tf_op jit(solution)/shard_map/all_to_all | solution.py:151
  10.0 10.2 %all-to-all-done = f32[16,16,512]{2,1,0:T(8,128)S(1)} async-done(((f32[16,16,512]{2,1,0:T(8,128)}), f32[16,16,512]{2,1,0:T(8,128)S(1)}, u32[]{:S(2)}, u32[]{:S(2)}) %all-to-all-start) | async-done | bytes 524320 | tf_op jit(solution)/shard_map/all_to_all | solution.py:151
  20.2 1.9 collective-permute-start
  22.1 3.3 collective-permute-done
  26.2 15.8 %all-to-all-start.1 = ((f32[8,16,512]{2,1,0:T(8,128)}), f32[8,16,512]{2,1,0:T(8,128)S(1)}, u32[]{:S(2)}, u32[]{:S(2)}) async-start(f32[8,16,512]{2,1,0:T(8,128)} %broadcast_in_dim.133), calls=%async_computation.1 | async-start | bytes 524288 | tf_op jit(solution)/shard_map/all_to_all | solution.py:151
  42.1 10.3 %all-to-all-done.1 = f32[8,16,512]{2,1,0:T(8,128)S(1)} async-done(((f32[8,16,512]{2,1,0:T(8,128)}), f32[8,16,512]{2,1,0:T(8,128)S(1)}, u32[]{:S(2)}, u32[]{:S(2)}) %all-to-all-start.1) | async-done | bytes 262176 | tf_op jit(solution)/shard_map/all_to_all | solution.py:151
  52.5 1.5 collective-permute-done.1
  55.7 32.5 %all_to_all.60 = f32[16,128,256]{2,1,0:T(8,128)S(1)} all-to-all(f32[16,128,256]{2,1,0:T(8,128)S(1)} %pad_maximum_fusion), channel_id=1, replica_groups=mesh['row'=16,'col_0'=8,'col_1'=2] {'row'}, dimensions={0} | all-to-all | bytes 4194304 | tf_op jit(solution)/shard_map/all_to_all | solution.py:151
  88.2 0.9 slice_reduce_fusion
  90.0 3.6 %all-to-all-start.4 = ((f32[16,32,256]{2,1,0:T(8,128)}), f32[16,32,256]{2,1,0:T(8,128)S(1)}, u32[]{:S(2)}, u32[]{:S(2)}) async-start(f32[16,32,256]{2,1,0:T(8,128)} %broadcast_in_dim.142), calls=%async_computation.4 | async-start | bytes 1048576 | tf_op jit(solution)/shard_map/all_to_all | solution.py:151
  93.6 3.3 collective-permute-start.2
  96.9 2.3 collective-permute-done.2
  99.2 11.0 %all-to-all-done.4.pieces_ref = f32[16,32,256]{2,1,0:T(8,128)S(1)} async-done(((f32[16,32,256]{2,1,0:T(8,128)}), f32[16,32,256]{2,1,0:T(8,128)S(1)}, u32[]{:S(2)}, u32[]{:S(2)}) %all-to-all-start.4) | async-done | bytes 524320 | tf_op jit(solution)/shard_map/all_to_all | solution.py:151
  110.1 1.0 broadcast_in_dim.141
  111.1 5.5 %all-to-all-start.3 = ((f32[8,2,16,512]{3,2,1,0:T(8,128)}), f32[8,2,16,512]{3,2,1,0:T(8,128)S(1)}, u32[]{:S(2)}, u32[]{:S(2)}) async-start(f32[8,2,16,512]{3,2,1,0:T(8,128)} %broadcast_in_dim.141), calls=%async_computation.3 | async-start | bytes 1048576 | tf_op jit(solution)/shard_map/all_to_all | solution.py:151
  116.7 0.9 reshape.225
  117.6 1.8 fusion.77
  120.2 1.2 reshape.223
  121.5 1.3 copy.66
  123.5 19.1 %factor.2 = (f32[256,256]{1,0:T(8,128)}, f32[256,256]{1,0:T(8,128)}, f32[256,256]{1,0:T(8,128)}) custom-call(f32[16,32,256]{2,1,0:T(8,128)} %copy-done.13), custom_call_target="tpu_custom_call" | custom-call | tf_op jit(solution)/shard_map/factor/pallas_call | solution.py:138
  142.5 2.0 copy.52
  144.5 0.9 convolution_add_fusion.2
  146.7 0.9 collective-permute-done.3
  148.5 6.7 %all-to-all-start.5 = ((f32[8,64,256]{2,1,0:T(8,128)}), f32[8,64,256]{2,1,0:T(8,128)}, u32[]{:S(2)}, u32[]{:S(2)}) async-start(f32[8,64,256]{2,1,0:T(8,128)} %broadcast_in_dim.145), calls=%async_computation.5 | async-start | bytes 1048576 | tf_op jit(solution)/shard_map/all_to_all | solution.py:151
  156.3 16.8 %all-to-all-done.5 = f32[8,64,256]{2,1,0:T(8,128)} async-done(((f32[8,64,256]{2,1,0:T(8,128)}), f32[8,64,256]{2,1,0:T(8,128)}, u32[]{:S(2)}, u32[]{:S(2)}) %all-to-all-start.5) | async-done | bytes 524320 | tf_op jit(solution)/shard_map/all_to_all | solution.py:151
  173.1 1.1 reduce_sum.56
  174.2 1.2 broadcast_in_dim.146
  175.4 10.5 %all-to-all-start.6 = ((f32[16,80,256]{2,1,0:T(8,128)}), f32[16,80,256]{2,1,0:T(8,128)}, u32[]{:S(2)}, u32[]{:S(2)}) async-start(f32[16,80,256]{2,1,0:T(8,128)} %broadcast_in_dim.146), calls=%async_computation.6 | async-start | bytes 2621440 | tf_op jit(solution)/shard_map/all_to_all | solution.py:151
  186.8 1.2 copy.55
  188.1 1.2 select_bitcast_fusion.1
  190.6 1.2 fusion.84
  191.8 13.1 %all-to-all-done.6 = f32[16,80,256]{2,1,0:T(8,128)} async-done(((f32[16,80,256]{2,1,0:T(8,128)}), f32[16,80,256]{2,1,0:T(8,128)}, u32[]{:S(2)}, u32[]{:S(2)}) %all-to-all-start.6) | async-done | bytes 1310752 | tf_op jit(solution)/shard_map/all_to_all | solution.py:151
  204.9 2.0 fusion.75
  207.6 1.9 slice.153
  209.4 2.0 reshape.228
  211.4 2.3 fusion.82
  213.7 1.3 fusion.83
  215.9 1.8 fusion.4
  219.2 6.6 %all-to-all-start.8 = ((f32[16,32,256]{2,1,0:T(8,128)}), f32[16,32,256]{2,1,0:T(8,128)}, u32[]{:S(2)}, u32[]{:S(2)}) async-start(f32[16,32,256]{2,1,0:T(8,128)} %broadcast_in_dim.150), calls=%async_computation.8 | async-start | bytes 1048576 | tf_op jit(solution)/shard_map/all_to_all | solution.py:151
  225.7 1.6 convolution_subtract_fusion.7
  227.3 3.1 convolution_subtract_fusion.1
  230.4 4.8 %all-to-all-done.8 = f32[16,32,256]{2,1,0:T(8,128)} async-done(((f32[16,32,256]{2,1,0:T(8,128)}), f32[16,32,256]{2,1,0:T(8,128)}, u32[]{:S(2)}, u32[]{:S(2)}) %all-to-all-start.8) | async-done | bytes 524320 | tf_op jit(solution)/shard_map/all_to_all | solution.py:151
  235.2 1.1 reduce_sum.57
  237.2 4.4 %all-to-all-start.9 = ((f32[16,32,256]{2,1,0:T(8,128)}), f32[16,32,256]{2,1,0:T(8,128)}, u32[]{:S(2)}, u32[]{:S(2)}) async-start(f32[16,32,256]{2,1,0:T(8,128)} %broadcast_in_dim.151), calls=%async_computation.9 | async-start | bytes 1048576 | tf_op jit(solution)/shard_map/all_to_all | solution.py:151
  241.5 1.4 fusion.85
  243.0 1.1 reshape.233
  244.7 1.2 fusion.6
  246.0 1.1 pad_maximum_fusion.3
  247.1 10.4 %all-to-all-done.9.pieces_ref = f32[16,32,256]{2,1,0:T(8,128)} async-done(((f32[16,32,256]{2,1,0:T(8,128)}), f32[16,32,256]{2,1,0:T(8,128)}, u32[]{:S(2)}, u32[]{:S(2)}) %all-to-all-start.9) | async-done | bytes 524320 | tf_op jit(solution)/shard_map/all_to_all | solution.py:151
  257.5 5.7 %all-to-all-start.7 = ((f32[16,64,256]{2,1,0:T(8,128)}), f32[16,64,256]{2,1,0:T(8,128)}, u32[]{:S(2)}, u32[]{:S(2)}) async-start(f32[16,64,256]{2,1,0:T(8,128)} %pad_maximum_fusion.3), calls=%async_computation.7 | async-start | bytes 2097152 | tf_op jit(solution)/shard_map/all_to_all | solution.py:151
  263.2 1.4 fusion.5
  264.6 19.0 %factor.3 = (f32[256,256]{1,0:T(8,128)}, f32[256,256]{1,0:T(8,128)}, f32[256,256]{1,0:T(8,128)}) custom-call(f32[16,32,256]{2,1,0:T(8,128)} %all-to-all-done.9.pieces_ref), custom_call_target="tpu_custom_call" | custom-call | tf_op jit(solution)/shard_map/factor/pallas_call | solution.py:138
  283.6 1.3 slice_reduce_fusion.2
  286.1 3.5 %collective-permute-start.5 = (f32[16,512]{1,0:T(8,128)S(1)}, f32[16,512]{1,0:T(8,128)S(1)}, u32[]{:S(2)}, u32[]{:S(2)}) collective-permute-start(f32[16,512]{1,0:T(8,128)S(1)} %convolution_add_fusion.1), channel_id=1, source_target_pairs={{0,0},{1,16},{2,32},{3,48},{4,64},{5,80},{6,96},{7,112},{8,128},{9... | collective-permute-start | bytes 98312 | tf_op jit(solution)/shard_map/ppermute | solution.py:167
  290.0 1.2 collective-permute-done.6
  292.2 11.4 %all-to-all-start.10 = ((f32[8,24,512]{2,1,0:T(8,128)}), f32[8,24,512]{2,1,0:T(8,128)S(1)}, u32[]{:S(2)}, u32[]{:S(2)}) async-start(f32[8,24,512]{2,1,0:T(8,128)} %broadcast_in_dim.154), calls=%async_computation.10 | async-start | bytes 786432 | tf_op jit(solution)/shard_map/all_to_all | solution.py:151
  303.7 14.8 %all-to-all-done.10 = f32[8,24,512]{2,1,0:T(8,128)S(1)} async-done(((f32[8,24,512]{2,1,0:T(8,128)}), f32[8,24,512]{2,1,0:T(8,128)S(1)}, u32[]{:S(2)}, u32[]{:S(2)}) %all-to-all-start.10) | async-done | bytes 393248 | tf_op jit(solution)/shard_map/all_to_all | solution.py:151
  318.6 1.0 broadcast_in_dim.155
  319.6 8.3 %all-to-all-start.11 = ((f32[16,48,256]{2,1,0:T(8,128)}), f32[16,48,256]{2,1,0:T(8,128)S(1)}, u32[]{:S(2)}, u32[]{:S(2)}) async-start(f32[16,48,256]{2,1,0:T(8,128)} %broadcast_in_dim.155), calls=%async_computation.11 | async-start | bytes 1572864 | tf_op jit(solution)/shard_map/all_to_all | solution.py:151
  330.1 11.5 %all-to-all-done.11 = f32[16,48,256]{2,1,0:T(8,128)S(1)} async-done(((f32[16,48,256]{2,1,0:T(8,128)}), f32[16,48,256]{2,1,0:T(8,128)S(1)}, u32[]{:S(2)}, u32[]{:S(2)}) %all-to-all-start.11) | async-done | bytes 786464 | tf_op jit(solution)/shard_map/all_to_all | solution.py:151
  344.3 2.7 fusion.3
  347.0 2.8 reshape.242
  (171 shorter events, 22.1 us)
Async XLA Ops:
  0.0 41.9 %copy-start.16 = (f32[2,256,2,256]{3,2,1,0:T(2,128)S(1)}, f32[2,256,2,256]{3,2,1,0:T(2,128)}, u32[]{:S(2)}) copy-start(f32[2,256,2,256]{3,2,1,0:T(2,128)} %param.1) | copy-start | bytes 3145732
  2.5 17.6 %all-to-all-start = ((f32[16,16,512]{2,1,0:T(8,128)}), f32[16,16,512]{2,1,0:T(8,128)S(1)}, u32[]{:S(2)}, u32[]{:S(2)}) async-start(f32[16,16,512]{2,1,0:T(8,128)} %reshape.217), calls=%async_computation | async-start | bytes 1048576 | tf_op jit(solution)/shard_map/all_to_all | solution.py:151
  20.2 33.8 %copy-start.29 = (f32[16,16,512]{2,1,0:T(8,128)}, f32[16,16,512]{2,1,0:T(8,128)S(1)}, u32[]{:S(2)}) copy-start(f32[16,16,512]{2,1,0:T(8,128)S(1)} %all-to-all-done) | copy-start | bytes 1572868
  20.2 5.2 %collective-permute-start = (f32[16,512]{1,0:T(8,128)S(1)}, f32[16,512]{1,0:T(8,128)S(1)}, u32[]{:S(2)}, u32[]{:S(2)}) collective-permute-start(f32[16,512]{1,0:T(8,128)S(1)} %bitcast_select_fusion), channel_id=1, source_target_pairs={{0,0},{1,16},{2,32},{3,48},{4,64},{5,80},{6,96},{7,112},{8,128},{9... | collective-permute-start | bytes 98312 | tf_op jit(solution)/shard_map/ppermute | solution.py:167
  26.2 26.3 %all-to-all-start.1 = ((f32[8,16,512]{2,1,0:T(8,128)}), f32[8,16,512]{2,1,0:T(8,128)S(1)}, u32[]{:S(2)}, u32[]{:S(2)}) async-start(f32[8,16,512]{2,1,0:T(8,128)} %broadcast_in_dim.133), calls=%async_computation.1 | async-start | bytes 524288 | tf_op jit(solution)/shard_map/all_to_all | solution.py:151
  52.4 1.5 collective-permute-start.1
  90.0 20.2 %all-to-all-start.4 = ((f32[16,32,256]{2,1,0:T(8,128)}), f32[16,32,256]{2,1,0:T(8,128)S(1)}, u32[]{:S(2)}, u32[]{:S(2)}) async-start(f32[16,32,256]{2,1,0:T(8,128)} %broadcast_in_dim.142), calls=%async_computation.4 | async-start | bytes 1048576 | tf_op jit(solution)/shard_map/all_to_all | solution.py:151
  93.6 5.6 %collective-permute-start.2 = (f32[2,16,512]{2,1,0:T(8,128)S(1)}, f32[2,16,512]{2,1,0:T(8,128)S(1)}, u32[]{:S(2)}, u32[]{:S(2)}) collective-permute-start(f32[2,16,512]{2,1,0:T(8,128)S(1)} %pad_maximum_fusion.18), channel_id=1, source_target_pairs={{0,0},{1,16},{2,32},{3,48},{4,64},{5,80},{6,96},{7,112},{8,128},{9... | collective-permute-start | bytes 196616 | tf_op jit(solution)/shard_map/ppermute | solution.py:167
  110.1 10.1 %copy-start.13 = (f32[16,32,256]{2,1,0:T(8,128)}, f32[16,32,256]{2,1,0:T(8,128)S(1)}, u32[]{:S(2)}) copy-start(f32[16,32,256]{2,1,0:T(8,128)S(1)} %all-to-all-done.4.pieces_ref) | copy-start | bytes 1572868
  111.1 31.4 %all-to-all-start.3 = ((f32[8,2,16,512]{3,2,1,0:T(8,128)}), f32[8,2,16,512]{3,2,1,0:T(8,128)S(1)}, u32[]{:S(2)}, u32[]{:S(2)}) async-start(f32[8,2,16,512]{3,2,1,0:T(8,128)} %broadcast_in_dim.141), calls=%async_computation.3 | async-start | bytes 1048576 | tf_op jit(solution)/shard_map/all_to_all | solution.py:151
  120.2 25.3 %copy-start.23 = (f32[256,256]{0,1:T(8,128)S(1)}, f32[256,256]{0,1:T(8,128)}, u32[]{:S(2)}) copy-start(f32[256,256]{0,1:T(8,128)} %copy.65) | copy-start | bytes 786436
  121.5 27.0 %copy-start.1 = (f32[256,512]{1,0:T(8,128)}, f32[256,512]{1,0:T(8,128)S(1)}, u32[]{:S(2)}) copy-start(f32[256,512]{1,0:T(8,128)S(1)} %reshape.223) | copy-start | bytes 1572868
  142.5 2.0 copy-start.19
  145.5 9.9 %slice-start = ((f32[16,32,256]{2,1,0:T(8,128)}), f32[16,16,256]{2,1,0:T(8,128)S(1)}, s32[]{:S(2)}) async-start(f32[16,32,256]{2,1,0:T(8,128)} %copy-done.13), calls=%async_computation.12 | async-start | bytes 524288 | tf_op jit(solution)/shard_map/slice | solution.py:302
  145.5 10.0 %copy-start.14 = (f32[256,256]{1,0:T(8,128)S(1)}, f32[256,256]{1,0:T(8,128)}, u32[]{:S(2)}) copy-start(f32[256,256]{1,0:T(8,128)} %get-tuple-element.22) | copy-start | bytes 786436
  145.5 40.4 %copy-start.8 = (f32[256,256]{0,1:T(8,128)}, f32[256,256]{0,1:T(8,128)S(1)}, u32[]{:S(2)}) copy-start(f32[256,256]{0,1:T(8,128)S(1)} %select_add_fusion) | copy-start | bytes 786436
  145.6 10.0 %copy-start.25 = (f32[256,256]{1,0:T(8,128)S(1)}, f32[256,256]{1,0:T(8,128)}, u32[]{:S(2)}) copy-start(f32[256,256]{1,0:T(8,128)} %get-tuple-element.25) | copy-start | bytes 786436
  145.8 1.8 collective-permute-start.3
  148.5 24.7 %all-to-all-start.5 = ((f32[8,64,256]{2,1,0:T(8,128)}), f32[8,64,256]{2,1,0:T(8,128)}, u32[]{:S(2)}, u32[]{:S(2)}) async-start(f32[8,64,256]{2,1,0:T(8,128)} %broadcast_in_dim.145), calls=%async_computation.5 | async-start | bytes 1048576 | tf_op jit(solution)/shard_map/all_to_all | solution.py:151
  155.2 32.9 %collective-permute-start.4 = (f32[8,2,16,512]{3,2,1,0:T(8,128)}, f32[8,2,16,512]{3,2,1,0:T(8,128)}, u32[]{:S(2)}, u32[]{:S(2)}) collective-permute-start(f32[8,2,16,512]{3,2,1,0:T(8,128)} %copy-done.19), channel_id=1, source_target_pairs={{0,1},{1,0},{2,3},{3,2},{4,5},{5,4},{6,7},{7,6},{8,9},{9,8},{10,11... | collective-permute-start | bytes 1572872 | tf_op jit(solution)/shard_map/ppermute | solution.py:171
  156.3 59.1 %copy-start.6 = (f32[256,256]{1,0:T(8,128)}, f32[256,256]{1,0:T(8,128)S(1)}, u32[]{:S(2)}) copy-start(f32[256,256]{1,0:T(8,128)S(1)} %get-tuple-element.54) | copy-start | bytes 786436
  156.3 59.1 %copy-start.7 = (f32[256,256]{1,0:T(8,128)}, f32[256,256]{1,0:T(8,128)S(1)}, u32[]{:S(2)}) copy-start(f32[256,256]{1,0:T(8,128)S(1)} %get-tuple-element.55) | copy-start | bytes 786436
  175.4 12.6 %copy-start.20 = (f32[8,2,16,512]{3,2,1,0:T(8,128)S(1)}, f32[8,2,16,512]{3,2,1,0:T(8,128)}, u32[]{:S(2)}) copy-start(f32[8,2,16,512]{3,2,1,0:T(8,128)} %copy-done.19) | copy-start | bytes 1572868
  175.4 29.5 %all-to-all-start.6 = ((f32[16,80,256]{2,1,0:T(8,128)}), f32[16,80,256]{2,1,0:T(8,128)}, u32[]{:S(2)}, u32[]{:S(2)}) async-start(f32[16,80,256]{2,1,0:T(8,128)} %broadcast_in_dim.146), calls=%async_computation.6 | async-start | bytes 2621440 | tf_op jit(solution)/shard_map/all_to_all | solution.py:151
  189.3 1.0 copy-start.15
  189.4 1.2 copy-start
  211.4 3.6 %copy-start.11 = (f32[256,256]{1,0:T(8,128)S(1)}, f32[256,256]{1,0:T(8,128)}, u32[]{:S(2)}) copy-start(f32[256,256]{1,0:T(8,128)} %get-tuple-element.69) | copy-start | bytes 786436
  211.4 4.0 %copy-start.21 = (f32[256,512]{1,0:T(8,128)S(1)}, f32[256,512]{1,0:T(8,128)}, u32[]{:S(2)}) copy-start(f32[256,512]{1,0:T(8,128)} %fusion.84) | copy-start | bytes 1572868
  215.4 2.3 copy-start.17
  215.9 1.9 copy-start.3
  219.2 16.1 %all-to-all-start.8 = ((f32[16,32,256]{2,1,0:T(8,128)}), f32[16,32,256]{2,1,0:T(8,128)}, u32[]{:S(2)}, u32[]{:S(2)}) async-start(f32[16,32,256]{2,1,0:T(8,128)} %broadcast_in_dim.150), calls=%async_computation.8 | async-start | bytes 1048576 | tf_op jit(solution)/shard_map/all_to_all | solution.py:151
  225.7 1.6 copy-start.4
  230.4 11.1 %copy-start.9 = (f32[512,512]{1,0:T(8,128)S(1)}, f32[512,512]{1,0:T(8,128)}, u32[]{:S(2)}) copy-start(f32[512,512]{1,0:T(8,128)} %convolution_subtract_fusion.1) | copy-start | bytes 3145732
  237.2 7.0 %copy-start.28 = (f32[16,16,256]{2,1,0:T(8,128)S(1)}, f32[16,16,256]{2,1,0:T(8,128)}, u32[]{:S(2)}) copy-start(f32[16,16,256]{2,1,0:T(8,128)} %get-tuple-element.37) | copy-start | bytes 786436
  237.2 20.3 %all-to-all-start.9 = ((f32[16,32,256]{2,1,0:T(8,128)}), f32[16,32,256]{2,1,0:T(8,128)}, u32[]{:S(2)}, u32[]{:S(2)}) async-start(f32[16,32,256]{2,1,0:T(8,128)} %broadcast_in_dim.151), calls=%async_computation.9 | async-start | bytes 1048576 | tf_op jit(solution)/shard_map/all_to_all | solution.py:151
  245.9 17.2 %copy-start.2 = (f32[256,512]{1,0:T(8,128)S(1)}, f32[256,512]{1,0:T(8,128)}, u32[]{:S(2)}) copy-start(f32[256,512]{1,0:T(8,128)} %copy-done.1) | copy-start | bytes 1572868
  246.0 17.2 %copy-start.12 = (f32[256,256]{1,0:T(8,128)S(1)}, f32[256,256]{1,0:T(8,128)}, u32[]{:S(2)}) copy-start(f32[256,256]{1,0:T(8,128)} %get-tuple-element.69) | copy-start | bytes 786436
  246.0 17.2 %copy-start.18 = (f32[256,256]{1,0:T(8,128)S(1)}, f32[256,256]{1,0:T(8,128)}, u32[]{:S(2)}) copy-start(f32[256,256]{1,0:T(8,128)} %copy-done.17) | copy-start | bytes 786436
  257.5 26.1 %all-to-all-start.7 = ((f32[16,64,256]{2,1,0:T(8,128)}), f32[16,64,256]{2,1,0:T(8,128)}, u32[]{:S(2)}, u32[]{:S(2)}) async-start(f32[16,64,256]{2,1,0:T(8,128)} %pad_maximum_fusion.3), calls=%async_computation.7 | async-start | bytes 2097152 | tf_op jit(solution)/shard_map/all_to_all | solution.py:151
  264.6 20.5 %copy-start.22 = (f32[256,512]{1,0:T(8,128)S(1)}, f32[256,512]{1,0:T(8,128)}, u32[]{:S(2)}) copy-start(f32[256,512]{1,0:T(8,128)} %fusion.5) | copy-start | bytes 1572868
  283.6 1.5 copy-start.30
  286.1 5.2 %collective-permute-start.5 = (f32[16,512]{1,0:T(8,128)S(1)}, f32[16,512]{1,0:T(8,128)S(1)}, u32[]{:S(2)}, u32[]{:S(2)}) collective-permute-start(f32[16,512]{1,0:T(8,128)S(1)} %convolution_add_fusion.1), channel_id=1, source_target_pairs={{0,0},{1,16},{2,32},{3,48},{4,64},{5,80},{6,96},{7,112},{8,128},{9... | collective-permute-start | bytes 98312 | tf_op jit(solution)/shard_map/ppermute | solution.py:167
  290.0 1.2 collective-permute-start.6
  292.2 35.7 %copy-start.26 = (f32[256,256]{1,0:T(8,128)S(1)}, f32[256,256]{1,0:T(8,128)}, u32[]{:S(2)}) copy-start(f32[256,256]{1,0:T(8,128)} %get-tuple-element.25) | copy-start | bytes 786436
  292.2 26.3 %all-to-all-start.10 = ((f32[8,24,512]{2,1,0:T(8,128)}), f32[8,24,512]{2,1,0:T(8,128)S(1)}, u32[]{:S(2)}, u32[]{:S(2)}) async-start(f32[8,24,512]{2,1,0:T(8,128)} %broadcast_in_dim.154), calls=%async_computation.10 | async-start | bytes 786432 | tf_op jit(solution)/shard_map/all_to_all | solution.py:151
  303.6 25.1 %copy-start.31 = (f32[256,256]{1,0:T(8,128)S(1)}, f32[256,256]{1,0:T(8,128)}, u32[]{:S(2)}) copy-start(f32[256,256]{1,0:T(8,128)} %get-tuple-element.29) | copy-start | bytes 786436
  318.5 11.1 %collective-permute-start.7 = (f32[8,16,512]{2,1,0:T(8,128)S(1)}, f32[8,16,512]{2,1,0:T(8,128)S(1)}, u32[]{:S(2)}, u32[]{:S(2)}) collective-permute-start(f32[8,16,512]{2,1,0:T(8,128)S(1)} %slice.162), channel_id=1, source_target_pairs={{0,1},{1,0},{2,3},{3,2},{4,5},{5,4},{6,7},{7,6},{8,9},{9,8},{10,11... | collective-permute-start | bytes 786440 | tf_op jit(solution)/shard_map/ppermute | solution.py:171
  319.6 10.1 %copy-start.5 = (f32[256,256]{1,0:T(8,128)S(1)}, f32[256,256]{1,0:T(8,128)}, u32[]{:S(2)}) copy-start(f32[256,256]{1,0:T(8,128)} %get-tuple-element.30) | copy-start | bytes 786436
  319.6 22.0 %all-to-all-start.11 = ((f32[16,48,256]{2,1,0:T(8,128)}), f32[16,48,256]{2,1,0:T(8,128)S(1)}, u32[]{:S(2)}, u32[]{:S(2)}) async-start(f32[16,48,256]{2,1,0:T(8,128)} %broadcast_in_dim.155), calls=%async_computation.11 | async-start | bytes 1572864 | tf_op jit(solution)/shard_map/all_to_all | solution.py:151
  342.4 1.0 copy-start.24
  342.8 1.2 copy-start.10
  342.8 1.3 copy-start.27
  342.8 1.3 copy-start.32
  342.9 1.4 copy-start.33
  342.9 1.5 copy-start.34
